TPU v7x, 32 devices: a whole 2x2x4 slice. The times are simulated.
32 devices in a mesh: groups: 2 (over x), epoch: 4 (over y, core), param: 4 (over z).
Axes of the slice: x: 2, y: 2, z: 4, core: 2. Of those that a mesh axis runs over, the one named last changes fastest.
Arguments:
- probes: bfloat16 [128, 65536], P(('groups', 'epoch'), 'param'), parts along dimension 0, may hold values from -0.0234375 to 0.0234375
- lat_bin: int32 [4096], P('epoch'), may hold values from 0 to 254
- lat_frac: float32 [4096], P('epoch'), may hold values from 0 to 1
- longitude: float32 [4096], P('epoch'), may hold values from -3.140625 to 3.140625
- order_code: int32 [65536], P('param'), may hold values from 0 to 511
- legendre: bfloat16 [256, 65536], P(None, 'param'), may hold values from -6 to 6
- bank: float32 [8, 255], replicated, may hold values from -0.01171875 to 0.01171875
- seg_filter: int32 [16], P('epoch'), may hold values from 0 to 7
Outputs:
- residual: float32 [128, 65536], P(('groups', 'epoch'), 'param'), parts along dimension 0
There are 2 independent parts, one for each index of `groups`. A program takes and returns all parts, laid end to end along the dimension named above; an argument that names none is the same for every part. Nothing has to cross between parts.
All inputs are finite; a program needn't handle non-finite values.
Results may differ from a plain program's by a relative error of at most 0.0061.
Values may be sent and summed in bfloat16 or wider, within the bound.
No kernel may reach another device: no remote copies, remote signals or barrier semaphores. Data moves between devices by JAX's collectives and lax.ppermute only.
A program may use at most 192 MiB of HBM per device.

v0:
```python
import jax
import jax.numpy as jnp
from jax import lax
from jax.sharding import PartitionSpec as P

TAPS = 255
SEG = 256
BLK = 128
TILE = 256
HALO = 256


HALF_PI = 1.5707963267948966


def passed_along(array, axis, by):
    devices = lax.axis_size(axis)
    pairs = [(i, i + by) for i in range(devices) if 0 <= i + by < devices]
    return lax.ppermute(array, axis, pairs)


def local(probes, lat_bin, lat_frac, longitude, order_code, legendre, bank, seg_filter):
    local_epochs = lat_bin.shape[0]
    kbins = legendre.shape[0]
    orders = (order_code // 2).astype(jnp.float32)
    is_sine = (order_code % 2).astype(jnp.float32)
    node_index = jnp.arange(kbins, dtype=jnp.int32)

    def design_tile(first_row):
        bins = lax.dynamic_slice_in_dim(lat_bin, first_row, TILE, 0)
        fraction = lax.dynamic_slice_in_dim(lat_frac, first_row, TILE, 0)
        angles = lax.dynamic_slice_in_dim(longitude, first_row, TILE, 0)
        lower_part = jnp.where(node_index[None, :] == bins[:, None], (1.0 - fraction)[:, None], 0.0)
        upper_part = jnp.where(node_index[None, :] == bins[:, None] + 1, fraction[:, None], 0.0)
        weights = (lower_part + upper_part).astype(jnp.bfloat16)
        interp = jnp.dot(weights, legendre, preferred_element_type=jnp.float32)
        phases = jnp.cos(angles[:, None] * orders[None, :] - is_sine[None, :] * HALF_PI)
        return (interp * phases).astype(jnp.bfloat16)

    tile_count = local_epochs // TILE
    tile_starts = jnp.arange(tile_count, dtype=jnp.int32) * TILE
    design = lax.map(design_tile, tile_starts).reshape(local_epochs, order_code.shape[0])
    partial_pred = lax.dot_general(
        lax.all_gather(probes, "epoch", axis=0, tiled=True),
        design,
        (((1,), (1,)), ((), ())),
        preferred_element_type=jnp.float32,
    )
    window_len = BLK + HALO
    block_count = local_epochs // BLK
    out_pos = jnp.arange(BLK, dtype=jnp.int32)
    win_pos = jnp.arange(window_len, dtype=jnp.int32)
    lag_table = out_pos[None, :] + HALO - win_pos[:, None]
    valid_lag = (lag_table >= 0) & (lag_table < TAPS)
    toeplitz = jnp.where(
        valid_lag[None, :, :], jnp.take(bank, jnp.clip(lag_table, 0, TAPS - 1), axis=1), 0.0
    )
    block_filter = seg_filter[jnp.arange(block_count, dtype=jnp.int32) * BLK // SEG]
    chosen = toeplitz[block_filter]
    share = lax.psum_scatter(partial_pred, "param", scatter_dimension=0, tiled=True)
    tail_cols = share[:, local_epochs - HALO :]
    before = passed_along(tail_cols, "epoch", 1)
    padded = jnp.concatenate([before, share], axis=1)

    def window_of(block_index):
        return lax.dynamic_slice_in_dim(padded, block_index * BLK, window_len, 1)

    windows = jax.vmap(window_of)(jnp.arange(block_count, dtype=jnp.int32))
    blocks = jnp.einsum(
        "brw,bwc->rbc",
        windows,
        chosen,
        precision=lax.Precision.HIGHEST,
        preferred_element_type=jnp.float32,
    )
    filtered = lax.all_gather(
        blocks.reshape(share.shape[0], local_epochs).astype(jnp.bfloat16),
        "param",
        axis=0,
        tiled=True,
    )
    return lax.psum_scatter(
        jnp.dot(filtered, design, preferred_element_type=jnp.float32),
        "epoch",
        scatter_dimension=0,
        tiled=True,
    )


def solution(mesh):
    placed = (
        P(("groups", "epoch"), "param"),
        P("epoch"),
        P("epoch"),
        P("epoch"),
        P("param"),
        P(None, "param"),
        P(),
        P("epoch"),
    )
    return jax.shard_map(
        local,
        mesh=mesh,
        in_specs=placed,
        out_specs=P(("groups", "epoch"), "param"),
        check_vma=False,
    )
```

profile of v0, /device:TPU:0, one launch (start us, length us, event | category | flops | bytes accessed | tf_op | source)
XLA Modules:
  0.0 586.6 jit_solution(11722415229974985914)
XLA Ops:
  6.5 0.7 all-gather.2.cloned.1.call-update
  7.3 0.9 fusion.21
  8.2 253.9 %while.14 = (s32[]{:T(128)}, bf16[4,256,16384]{2,1,0:T(8,128)(2,1)}, s32[4]{0:T(128)S(1)}, s32[1024]{0:T(1024)}, f32[1024]{0:T(1024)}, /*index=5*/bf16[256,16384...) while((s32[]{:T(128)}, ...), condition=%wide.region_1.2_spmd.clone.clone, body=%wide.region_0.1_spmd.clone.clone.sunk | while | flops 2164670976 | bytes 17315504 | solution.py:42
  8.3 0.6 dynamic_slice.29
  10.8 0.8 broadcast_subtract_fusion.2
  11.6 0.8 broadcast_add_fusion.2
  12.3 0.2 add_convert_fusion.6
  12.5 0.8 dynamic_slice.30
  13.3 58.4 %fusion.41 = bf16[4,256,16384]{2,1,0:T(8,128)(2,1)} fusion(bf16[4,256,16384]{2,1,0:T(8,128)(2,1)} %get-tuple-element.248, s32[]{:T(128)} %get-tuple-element.247, bf16[256,16384]{1,0:T(8,128)(2,1)} %get-tuple-element.264, f32[16384]{0:T(1024)S(1)} %broadcast_multiply_fusion.2, f32[16384]{0:T(1024)S(1)} %get-tuple-element.266, ...), kind=kOutput, calls=%fused_computation.9.clone.2 | convolution fusion | flops 2164260864 | bytes 17040896 | tf_op jit(solution)/shard_map/while/body/eval_jaxpr/dot_general | solution.py:36
  71.7 0.6 dynamic_slice.29
  74.3 0.8 broadcast_subtract_fusion.2
  75.0 0.8 broadcast_add_fusion.2
  75.8 0.2 add_convert_fusion.6
  76.0 0.8 dynamic_slice.30
  76.8 58.4 %fusion.41 = bf16[4,256,16384]{2,1,0:T(8,128)(2,1)} fusion(bf16[4,256,16384]{2,1,0:T(8,128)(2,1)} %get-tuple-element.248, s32[]{:T(128)} %get-tuple-element.247, bf16[256,16384]{1,0:T(8,128)(2,1)} %get-tuple-element.264, f32[16384]{0:T(1024)S(1)} %broadcast_multiply_fusion.2, f32[16384]{0:T(1024)S(1)} %get-tuple-element.266, ...), kind=kOutput, calls=%fused_computation.9.clone.2 | convolution fusion | flops 2164260864 | bytes 17040896 | tf_op jit(solution)/shard_map/while/body/eval_jaxpr/dot_general | solution.py:36
  135.2 0.6 dynamic_slice.29
  137.7 0.8 broadcast_subtract_fusion.2
  138.5 0.8 broadcast_add_fusion.2
  139.3 0.2 add_convert_fusion.6
  139.5 0.8 dynamic_slice.30
  140.2 58.4 %fusion.41 = bf16[4,256,16384]{2,1,0:T(8,128)(2,1)} fusion(bf16[4,256,16384]{2,1,0:T(8,128)(2,1)} %get-tuple-element.248, s32[]{:T(128)} %get-tuple-element.247, bf16[256,16384]{1,0:T(8,128)(2,1)} %get-tuple-element.264, f32[16384]{0:T(1024)S(1)} %broadcast_multiply_fusion.2, f32[16384]{0:T(1024)S(1)} %get-tuple-element.266, ...), kind=kOutput, calls=%fused_computation.9.clone.2 | convolution fusion | flops 2164260864 | bytes 17040896 | tf_op jit(solution)/shard_map/while/body/eval_jaxpr/dot_general | solution.py:36
  198.7 0.6 dynamic_slice.29
  201.2 0.8 broadcast_subtract_fusion.2
  202.0 0.8 broadcast_add_fusion.2
  202.7 0.2 add_convert_fusion.6
  202.9 0.8 dynamic_slice.30
  203.7 58.5 %fusion.41 = bf16[4,256,16384]{2,1,0:T(8,128)(2,1)} fusion(bf16[4,256,16384]{2,1,0:T(8,128)(2,1)} %get-tuple-element.248, s32[]{:T(128)} %get-tuple-element.247, bf16[256,16384]{1,0:T(8,128)(2,1)} %get-tuple-element.264, f32[16384]{0:T(1024)S(1)} %broadcast_multiply_fusion.2, f32[16384]{0:T(1024)S(1)} %get-tuple-element.266, ...), kind=kOutput, calls=%fused_computation.9.clone.2 | convolution fusion | flops 2164260864 | bytes 17040896 | tf_op jit(solution)/shard_map/while/body/eval_jaxpr/dot_general | solution.py:36
  262.2 0.1 copy.10
  262.3 0.1 fusion.13
  262.4 162.9 %gather_fusion = f32[49152,8]{1,0:T(8,128)} fusion(f32[8,255]{0,1:T(8,128)S(1)} %copy.10, s32[49152]{0:T(1024)S(1)} %fusion.13), kind=kCustom, calls=%fused_computation | custom fusion | bytes 3342336 | tf_op jit(solution)/shard_map/jit(_take)/gather | solution.py:56
  425.3 18.1 %copy.11 = f32[384,128,8]{0,1,2:T(8,128)S(1)} copy(f32[384,128,8]{2,1,0:T(8,128)} %bitcast.54) | data formatting | bytes 3145728 | tf_op jit(solution)/shard_map/jit(_take)/gather | solution.py:56
  443.5 0.6 gather_fusion.1
  444.1 22.1 %convolution_bitcast_fusion = f32[64,1024]{1,0:T(8,128)} fusion(bf16[1024,16384]{1,0:T(8,128)(2,1)} %bitcast.52, bf16[64,16384]{1,0:T(8,128)(2,1)} %all-gather.2.cloned.1.call-done), kind=kOutput, calls=%fused_computation.23 | convolution fusion | flops 2147483648 | bytes 35913728 | tf_op jit(solution)/shard_map/dot_general | solution.py:43
  466.3 0.2 fusion.18
  466.5 0.2 select_bitcast_fusion
  466.7 22.5 %reduce-scatter.3.cloned.1.call-done = f32[16,1024]{1,0:T(8,128)} async-done(((f32[64,1024]{1,0:T(8,128)}), f32[16,1024]{1,0:T(8,128)}) %reduce-scatter.3.cloned.1.call-update) | async-done | bytes 65552 | tf_op jit(solution)/shard_map/reduce_scatter | solution.py:60
  489.1 0.7 slice.21
  489.9 1.3 collective-permute-start
  491.2 0.7 gather_fusion.2
  491.8 0.1 collective-permute-done
  492.0 0.8 pad_maximum_fusion
  492.8 10.5 %while.13 = (s32[]{:T(128)}, f32[16,1280]{1,0:T(8,128)S(1)}, s32[8,2]{0,1:T(2,128)S(1)}, f32[8,16,384]{2,1,0:T(8,128)S(1)}, s32[]{:T(128)}) while((s32[]{:T(128)}, f32[16,1280]{1,0:T(8,128)S(1)}, s32[8,2]{0,1:T(2,128)S(1)}, f32[8,16,384]{2,1,0:T(8,128)S(1)}, s32[]{:T(128)}) %tuple.46), condition=%wide.while_cond, body=%wide.while_body.sunk | while | flops 2 | bytes 49249 | solution.py:66
  492.8 0.1 constant_dynamic-slice_fusion.2
  492.9 0.5 slice.23
  493.4 0.7 bitcast_dynamic-update-slice_fusion.2
  494.1 0.1 constant_dynamic-slice_fusion.2
  494.2 0.5 slice.23
  494.7 0.7 bitcast_dynamic-update-slice_fusion.2
  495.5 0.5 slice.23
  496.0 0.7 bitcast_dynamic-update-slice_fusion.2
  496.8 0.5 slice.23
  497.3 0.7 bitcast_dynamic-update-slice_fusion.2
  498.1 0.5 slice.23
  498.6 0.7 bitcast_dynamic-update-slice_fusion.2
  499.4 0.5 slice.23
  500.0 0.7 bitcast_dynamic-update-slice_fusion.2
  500.8 0.5 slice.23
  501.3 0.7 bitcast_dynamic-update-slice_fusion.2
  502.1 0.5 slice.23
  502.6 0.7 bitcast_dynamic-update-slice_fusion.2
  503.3 1.8 fusion.11
  505.1 13.4 %all_gather.7 = bf16[64,1024]{1,0:T(8,128)(2,1)S(1)} all-gather(bf16[16,1024]{1,0:T(8,128)(2,1)S(1)} %bitcast.55), channel_id=1, replica_groups=mesh['groups'=2,'epoch'=4,'param'=4] {'param'}, dimensions={0}, use_global_device_ids=true | all-gather | bytes 163840 | tf_op jit(solution)/shard_map/all_gather | solution.py:76
  518.5 15.6 %fusion.26 = f32[64,16384]{1,0:T(8,128)} fusion(bf16[64,1024]{1,0:T(8,128)(2,1)S(1)} %all_gather.7, bf16[1024,16384]{1,0:T(8,128)(2,1)} %bitcast.53), kind=kOutput, calls=%fused_computation.63 | convolution fusion | flops 2147483648 | bytes 37879808 | tf_op jit(solution)/shard_map/dot_general | solution.py:83
  534.2 45.9 %reduce-scatter.5.cloned.1.call-done = f32[16,16384]{1,0:T(8,128)} async-done(((f32[64,16384]{1,0:T(8,128)}), f32[16,16384]{1,0:T(8,128)}) %reduce-scatter.5.cloned.1.call-update) | async-done | bytes 1048592 | tf_op jit(solution)/shard_map/reduce_scatter | solution.py:82
  (31 shorter events, 0.7 us)
Async XLA Ops:
  6.5 436.9 %copy-start = (s32[4]{0:T(128)S(1)}, s32[4]{0:T(128)}, u32[]{:S(2)}) copy-start(s32[4]{0:T(128)} %param.17) | copy-start | bytes 52
  6.5 437.6 %all-gather.2.cloned.1.call-start = ((), (), s32[]{:S(2)}) async-start(), calls=%async_computation.2 | async-start | bytes 2621440 | tf_op jit(solution)/shard_map/all_gather | solution.py:44
  7.3 481.9 %reduce-scatter.3.cloned.1.call-start = ((), (), s32[]{:S(2)}) async-start(), calls=%async_computation.3 | async-start | bytes 327680 | tf_op jit(solution)/shard_map/reduce_scatter | solution.py:60
  8.2 253.9 %copy-start.1 = (f32[8,255]{1,0:T(8,128)S(1)}, f32[8,255]{1,0:T(8,128)}, u32[]{:S(2)}) copy-start(f32[8,255]{1,0:T(8,128)} %param.16) | copy-start | bytes 24484
  466.3 113.8 %reduce-scatter.5.cloned.1.call-start = ((), (), s32[]{:S(2)}) async-start(), calls=%async_computation.4 | async-start | bytes 5242880 | tf_op jit(solution)/shard_map/reduce_scatter | solution.py:82
  489.9 2.1 collective-permute-start
Sparse Core Ops, SparseCore 0:
  8.9 25.2 all-gather.1
  466.4 22.7 reduce-scatter.2
  534.3 45.7 reduce-scatter.4
where the time goes:
time: 588 us; the launch traced here: 587 us
  matrix products  273 us (46%)
  local copies, waits for them, and re-layouts  199 us (34%)
  waiting for transfers between devices  69.2 us (12%)
  blocking collectives  13.4 us (2%)
  between operations  13.3 us (2%)
  other arithmetic  9.19 us (2%)
  loops' own time  7.74 us (1%)
    dot_general x4, matrix products, design_tile(): interp = jnp.dot(weights, legendre, preferred_element_type=jnp.float32)  234 us
    gather x2, local copies, waits for them, and re-layouts, local(): jnp.take(bank, jnp.clip(lag_table, 0, TAPS - 1), axis=1)  181 us
    reduce_scatter x1, waiting for transfers between devices, local(): lax.psum_scatter(jnp.dot(filtered, design, preferred_element_type=jnp.flo...  45.9 us
    reduce_scatter x1, waiting for transfers between devices, local(): lax.psum_scatter(partial_pred, 'param', scatter_dimension=0, tiled=True)  22.5 us
    dot_general x1, matrix products, local(): lax.dot_general(lax.all_gather(probes, 'epoch', axis=0, tiled=True), desi...  22.1 us
    dot_general x1, matrix products, local(): jnp.dot(filtered, design, preferred_element_type=jnp.float32)  15.6 us
    all_gather x1, blocking collectives, local(): lax.all_gather(blocks.reshape(share.shape[0], local_epochs).astype(jnp.bf...  13.4 us
  transfers between devices with their start and end apart: 4, of which 3 were waited for; matrix products, arithmetic and copies ran while one was open for 73% of the time, Pallas kernels for 0%

commit v1 on v0

v1 whole, which is shorter than its diff:
```python
import functools

import jax
import jax.numpy as jnp
from jax import lax
from jax.experimental import pallas as pl
from jax.experimental.pallas import tpu as pltpu
from jax.sharding import PartitionSpec as P

SEG = 256
ORDERS = 256
ROWS = 256
COLS = 1024
INV_TWO_PI = 0.15915494309189535
TWO_PI_HI = 6.28125
TWO_PI_LO = 0.0019353071795864769
COS = (1.0, -1 / 2, 1 / 24, -1 / 720, 1 / 40320, -1 / 3628800, 1 / 479001600, -1 / 87178291200, 1 / 20922789888000)
SIN = (1.0, -1 / 6, 1 / 120, -1 / 5040, 1 / 362880, -1 / 39916800, 1 / 6227020800, -1 / 1307674368000, 1 / 355687428096000)
BF16 = jnp.bfloat16
F32 = jnp.float32


def horner(coefficients, x):
    total = coefficients[-1]
    for coefficient in coefficients[-2::-1]:
        total = total * x + coefficient
    return total


def dot(a, b):
    return jnp.dot(a, b, preferred_element_type=F32)


def dot_t(a, b):
    return lax.dot_general(a, b, (((1,), (1,)), ((), ())), preferred_element_type=F32)


def column(row_ref):
    row = row_ref[...].astype(F32)
    return jnp.transpose(jnp.broadcast_to(row, (8, row.shape[1])))[:, :1]


def fill_tables(bin_ref, frac_ref, lon_ref, weights_ref, trig_ref):
    nodes = weights_ref.shape[1]
    bins, fraction, angles = column(bin_ref), column(frac_ref), column(lon_ref)
    node = lax.broadcasted_iota(jnp.int32, (1, nodes), 1).astype(F32)
    order = lax.broadcasted_iota(jnp.int32, (1, ORDERS), 1).astype(F32)
    for first in range(0, weights_ref.shape[0], ROWS):
        rows = slice(first, first + ROWS)
        b, f = bins[rows], fraction[rows]
        lower = jnp.where(node == b, 1.0 - f, 0.0)
        upper = jnp.where(node == b + 1.0, f, 0.0)
        weights_ref[rows, :] = (lower + upper).astype(BF16)
        angle = angles[rows] * order
        turns = jnp.round(angle * INV_TWO_PI)
        rest = (angle - turns * TWO_PI_HI) - turns * TWO_PI_LO
        square = rest * rest
        trig_ref[rows, :ORDERS] = horner(COS, square).astype(BF16)
        trig_ref[rows, ORDERS:] = (rest * horner(SIN, square)).astype(BF16)


def design_tile(weights_ref, trig_ref, code_ref, legendre_ref, rows, chosen):
    interp = dot(weights_ref[rows, :], legendre_ref[...])
    phases = dot(trig_ref[rows, :], chosen)
    return (interp * phases).astype(BF16)


def one_hot(code_ref):
    code = code_ref[...]
    place = lax.shift_right_logical(code, 1) + (code & 1) * ORDERS
    index = lax.broadcasted_iota(jnp.int32, (2 * ORDERS, 1), 0)
    return jnp.where(index == place, 1.0, 0.0).astype(BF16)


def first_kernel(bin_ref, frac_ref, lon_ref, code_ref, legendre_ref, design_ref, weights_ref, trig_ref):
    @pl.when(pl.program_id(0) == 0)
    def _():
        fill_tables(bin_ref, frac_ref, lon_ref, weights_ref, trig_ref)

    chosen = one_hot(code_ref)
    for first in range(0, design_ref.shape[0], ROWS):
        rows = slice(first, first + ROWS)
        design_ref[rows, :] = design_tile(weights_ref, trig_ref, code_ref, legendre_ref, rows, chosen)


def second_kernel(weights_ref, trig_ref, code_ref, legendre_ref, probes_ref, old_ref, old_probes_ref,
                  design_ref, pred_ref, sent_ref, total_ref):
    step = pl.program_id(0)

    @pl.when(step == 0)
    def _():
        total_ref[...] = jnp.zeros_like(total_ref)

    chosen = one_hot(code_ref)
    for first in range(0, design_ref.shape[0], ROWS):
        rows = slice(first, first + ROWS)
        tile = design_tile(weights_ref, trig_ref, code_ref, legendre_ref, rows, chosen)
        design_ref[rows, :] = tile
        total_ref[rows, :] += dot_t(tile, probes_ref[...]) + dot_t(old_ref[rows, :], old_probes_ref[...])

    @pl.when(step == pl.num_programs(0) - 1)
    def _():
        total = jnp.transpose(total_ref[...])
        pred_ref[...] = total
        sent_ref[...] = total.astype(BF16)


def filter_kernel(seg_ref, bank_ref, before_ref, pred_ref, out_ref):
    for segment in range(pred_ref.shape[1] // SEG):
        taps = bank_ref[pl.ds(seg_ref[segment], 1), :]
        spread = jnp.broadcast_to(taps, (2 * SEG, 2 * SEG))
        table = pltpu.roll(spread, SEG, 1, stride=1, stride_axis=0)[:, :SEG]
        here = pred_ref[:, segment * SEG : (segment + 1) * SEG]
        past = before_ref[...] if segment == 0 else pred_ref[:, (segment - 1) * SEG : segment * SEG]
        window = jnp.concatenate([past, here], axis=1)
        value = jnp.dot(window, table, precision=lax.Precision.HIGHEST, preferred_element_type=F32)
        out_ref[:, segment * SEG : (segment + 1) * SEG] = value.astype(BF16)


def residual_kernel(filtered_ref, design_ref, kept_ref, sent_ref):
    value = dot(filtered_ref[...], design_ref[...])
    half = kept_ref.shape[0]
    kept_ref[...] = value[:half]
    sent_ref[...] = value[half:].astype(BF16)


def struct(shape, dtype):
    return jax.ShapeDtypeStruct(shape, dtype)


def whole(shape):
    return pl.BlockSpec(shape, lambda c: (0,) * len(shape))


def across(rows, cols, shift=0):
    return pl.BlockSpec((rows, cols), lambda c: (0, c + shift))


def cost(flops, nbytes):
    return pl.CostEstimate(flops=flops, bytes_accessed=nbytes, transcendentals=0)


def swapped(array, axis, bit):
    size = lax.axis_size(axis)
    return lax.ppermute(array, axis, [(i, i ^ bit) for i in range(size)])


def bits_of(axis):
    return [1 << b for b in range(lax.axis_size(axis).bit_length() - 1)]


def local(probes, lat_bin, lat_frac, longitude, order_code, legendre, bank, seg_filter):
    epochs, (nodes, coeffs) = lat_bin.shape[0], legendre.shape
    own = probes.shape[0]
    epoch_bits = bits_of("epoch")
    row = lambda array: array.reshape(1, -1)
    codes = row(order_code)
    half = coeffs // 2
    cols = min(COLS, half)
    steps = half // cols

    gathered = probes
    for bit in reversed(epoch_bits):
        gathered = jnp.concatenate([gathered, swapped(gathered, "epoch", bit)], axis=0)
    count = gathered.shape[0]

    design_1, weights, trig = pl.pallas_call(
        first_kernel,
        grid=(steps,),
        in_specs=[whole((1, epochs))] * 3 + [across(1, cols), across(nodes, cols)],
        out_specs=[across(epochs, cols), whole((epochs, nodes)), whole((epochs, 2 * ORDERS))],
        out_shape=[struct((epochs, half), BF16), struct((epochs, nodes), BF16), struct((epochs, 2 * ORDERS), BF16)],
        cost_estimate=cost(2 * epochs * half * (nodes + 2 * ORDERS), 2 * half * (epochs + nodes)),
        name="design_first",
    )(row(lat_bin), row(lat_frac), row(longitude), codes, legendre)

    design_2, pred, sent = pl.pallas_call(
        second_kernel,
        grid=(steps,),
        in_specs=[
            whole((epochs, nodes)),
            whole((epochs, 2 * ORDERS)),
            across(1, cols, steps),
            across(nodes, cols, steps),
            across(count, cols, steps),
            across(epochs, cols),
            across(count, cols),
        ],
        out_specs=[across(epochs, cols), whole((count, epochs)), whole((count, epochs))],
        out_shape=[struct((epochs, half), BF16), struct((count, epochs), F32), struct((count, epochs), BF16)],
        scratch_shapes=[pltpu.VMEM((epochs, count), F32)],
        cost_estimate=cost(2 * epochs * half * (nodes + 2 * ORDERS + 2 * count), 2 * half * (2 * epochs + nodes)),
        name="design_second",
    )(weights, trig, codes, legendre, gathered, design_1, gathered)

    for bit in bits_of("param"):
        pred = pred + swapped(sent, "param", bit).astype(F32)
        sent = pred.astype(BF16)

    devices = lax.axis_size("epoch")
    before = lax.ppermute(pred[:, epochs - SEG :], "epoch", [(i, i + 1) for i in range(devices - 1)])
    here = lax.axis_index("epoch")
    differing = here ^ (here - 1)
    before = before.reshape((2,) * len(epoch_bits) + (own, SEG))
    for place, bit in enumerate(epoch_bits):
        before = jnp.where((differing & bit) != 0, jnp.flip(before, place), before)
    before = before.reshape(count, SEG)

    taps = jnp.pad(bank, ((0, 0), (0, 2 * SEG - bank.shape[1])))
    filtered = pl.pallas_call(
        filter_kernel,
        in_specs=[pl.BlockSpec(memory_space=pltpu.SMEM)] + [pl.BlockSpec(memory_space=pltpu.VMEM)] * 3,
        out_specs=pl.BlockSpec(memory_space=pltpu.VMEM),
        out_shape=struct((count, epochs), BF16),
        cost_estimate=cost(12 * count * epochs * 2 * SEG, 8 * count * epochs),
        name="filter",
    )(seg_filter, taps, before, pred)

    pieces = []
    for design in (design_1, design_2):
        kept, sent = pl.pallas_call(
            residual_kernel,
            grid=(steps,),
            in_specs=[whole((count, epochs)), across(epochs, cols)],
            out_specs=[across(count // 2, cols)] * 2,
            out_shape=[struct((count // 2, half), F32), struct((count // 2, half), BF16)],
            cost_estimate=cost(2 * count * epochs * half, 2 * epochs * half),
            name="residual",
        )(filtered, design)
        for bit in epoch_bits[:-1]:
            total = kept + swapped(sent, "epoch", bit).astype(F32)
            rows = total.shape[0] // 2
            kept, sent = total[:rows], total[rows:].astype(BF16)
        pieces.append(kept + swapped(sent, "epoch", epoch_bits[-1]).astype(F32))
    return jnp.concatenate(pieces, axis=1)


def solution(mesh):
    placed = (
        P(("groups", "epoch"), "param"),
        P("epoch"),
        P("epoch"),
        P("epoch"),
        P("param"),
        P(None, "param"),
        P(),
        P("epoch"),
    )
    return jax.shard_map(
        local,
        mesh=mesh,
        in_specs=placed,
        out_specs=P(("groups", "epoch"), "param"),
        check_vma=False,
    )
```

time: 588 us -> 129 us (0.22)
  matrix products: 273 us -> 0 us
  local copies, waits for them, and re-layouts: 199 us -> 0.69 us
  Pallas kernels: 0 us -> 72.2 us
  waiting for transfers between devices: 69.2 us -> 31.9 us
  starting transfers between devices: 1.36 us -> 16.2 us
  blocking collectives: 13.4 us -> 0 us
  between operations: 13.3 us -> 0.12 us
  loops' own time: 7.74 us -> 0 us
    dot_general x7 -> x0, matrix products: 273 us -> none  [the longest x4 234 us: design_tile(): interp = jnp.dot(weights, legendre, preferred_element_type=jnp.float32)]
    gather x28 -> x0, local copies, waits for them, and re-layouts: 193 us -> none  [the longest x2 181 us: local(): jnp.take(bank, jnp.clip(lag_table, 0, TAPS - 1), axis=1)]
    pallas_call x0 -> x5, Pallas kernels: none -> 72.2 us  [the longest x1 28.7 us: local(): pl.pallas_call(second_kernel, grid=(steps,), in_specs=[whole((epochs, nod...]
    reduce_scatter x2 -> x0, waiting for transfers between devices: 68.3 us -> none  [the longest x1 45.9 us: local(): lax.psum_scatter(jnp.dot(filtered, design, preferred_element_type=jnp.flo...]
    ppermute x1 -> x9, waiting for transfers between devices: 0.13 us -> 31.9 us  [the longest x8 31.7 us: swapped(): return lax.ppermute(array, axis, [(i, i ^ bit) for i in range(size)])]
    ppermute x1 -> x9, starting transfers between devices: 1.28 us -> 16.2 us  [the longest x8 14.9 us: swapped(): return lax.ppermute(array, axis, [(i, i ^ bit) for i in range(size)])]
    all_gather x1 -> x0, blocking collectives: 13.4 us -> none  [local(): lax.all_gather(blocks.reshape(share.shape[0], local_epochs).astype(jnp.bf...]
    another operation x2 -> x0, loops' own time: 7.74 us -> none  [the longest x1 7.73 us: local(): lax.map(design_tile, tile_starts).reshape(local_epochs, order_code.shape[0])]
  transfers between devices with their start and end apart: 4 -> 9, of which waited for: 3 -> 6; matrix products, arithmetic and copies ran while one was open for 73% -> 2% of each run, Pallas kernels for 0% -> 23%
where the time goes in v1:
time: 129 us
  Pallas kernels  72.2 us (56%)
  waiting for transfers between devices  31.9 us (25%)
  starting transfers between devices  16.2 us (13%)
  other arithmetic  7.73 us (6%)
    ppermute x8, waiting for transfers between devices, swapped(): return lax.ppermute(array, axis, [(i, i ^ bit) for i in range(size)])  31.7 us
    pallas_call x1, Pallas kernels, local(): pl.pallas_call(second_kernel, grid=(steps,), in_specs=[whole((epochs, nod...  28.7 us
    pallas_call x2, Pallas kernels, local(): pl.pallas_call(residual_kernel, grid=(steps,), in_specs=[whole((count, ep...  20.8 us
    pallas_call x1, Pallas kernels, local(): pl.pallas_call(first_kernel, grid=(steps,), in_specs=[whole((1, epochs))]...  19.7 us
    ppermute x8, starting transfers between devices, swapped(): return lax.ppermute(array, axis, [(i, i ^ bit) for i in range(size)])  14.9 us
    pallas_call x1, Pallas kernels, local(): pl.pallas_call(filter_kernel, in_specs=[pl.BlockSpec(memory_space=pltpu.S...  3.03 us
  transfers between devices with their start and end apart: 9, of which 6 were waited for; matrix products, arithmetic and copies ran while one was open for 2% of the time, Pallas kernels for 23%

profile of v1, /device:TPU:0, one launch (start us, length us, event | category | flops | bytes accessed | tf_op | source)
XLA Modules:
  0.0 128.9 jit_solution(9251274798646770797)
XLA Ops:
  0.0 3.0 %collective-permute-start = (bf16[16,16384]{1,0:T(8,128)(2,1)}, bf16[16,16384]{1,0:T(8,128)(2,1)S(1)}, u32[]{:S(2)}, u32[]{:S(2)}) collective-permute-start(bf16[16,16384]{1,0:T(8,128)(2,1)} %param.8), channel_id=1, source_target_pairs={{0,8},{4,12},{8,0},{12,4},{1,9},{5,13},{9,1},{13,5},{2,10},{6,14},... | collective-permute-start | bytes 1572872 | tf_op jit(solution)/shard_map/ppermute | solution.py:145
  3.0 12.1 %collective-permute-done = bf16[16,16384]{1,0:T(8,128)(2,1)S(1)} collective-permute-done((bf16[16,16384]{1,0:T(8,128)(2,1)}, bf16[16,16384]{1,0:T(8,128)(2,1)S(1)}, u32[]{:S(2)}, u32[]{:S(2)}) %collective-permute-start) | collective-permute-done | bytes 524320 | tf_op jit(solution)/shard_map/ppermute | solution.py:145
  15.1 1.1 pad_maximum_fusion.1
  16.2 0.1 collective-permute-start.1
  16.3 0.0 copy-start
  16.3 19.7 %design_first.1 = (bf16[1024,8192]{1,0:T(8,128)(2,1)}, bf16[1024,256]{1,0:T(8,128)(2,1)}, bf16[1024,512]{1,0:T(8,128)(2,1)}) custom-call(s32[1,1024]{1,0:T(1,128)} %bitcast.10, f32[1,1024]{1,0:T(1,128)} %bitcast.11, f32[1,1024]{1,0:T(1,128)} %bitcast.12, s32[1,16384]{1,0:T(1,128)} %bitcast.8, bf16[256,16384]{1,0:T(8,128)(2,1)} %legendre_ref.3), custom_call_target="tpu_custom_call" | custom-call | flops 12884901888 | bytes 20971520 | tf_op jit(solution)/shard_map/design_first/pallas_call | solution.py:167
  36.1 0.0 collective-permute-done.1
  36.1 0.0 copy-done
  36.1 1.5 %pad_maximum_fusion.probes_ref.old_probes_ref = bf16[64,16384]{1,0:T(8,128)(2,1)} fusion(bf16[32,16384]{1,0:T(8,128)(2,1)S(1)} %collective-permute-done.1, bf16[16,16384]{1,0:T(8,128)(2,1)S(1)} %collective-permute-done, bf16[16,16384]{1,0:T(8,128)(2,1)S(1)} %copy-done), kind=kLoop, calls=%fused_computation | loop fusion | flops 6291456 | bytes 4194304 | tf_op jit(solution)/shard_map/concatenate | solution.py:164
  37.5 0.0 copy-start.3
  37.5 28.7 %design_second.1 = (bf16[1024,8192]{1,0:T(8,128)(2,1)}, f32[64,1024]{1,0:T(8,128)}, bf16[64,1024]{1,0:T(8,128)(2,1)}) custom-call(bf16[1024,256]{1,0:T(8,128)(2,1)} %get-tuple-element.15.weights_ref, bf16[1024,512]{1,0:T(8,128)(2,1)} %get-tuple-element.16.trig_ref, s32[1,16384]{1,0:T(1,128)} %bitcast.9, bf16[256,16384]{1,0:T(8,128)(2,1)} %legendre_ref.3, ...), custom_call_target="tpu_custom_call" | custom-call | flops 15032385536 | bytes 37748736 | tf_op jit(solution)/shard_map/design_second/pallas_call | solution.py:177
  66.2 1.9 %collective-permute-start.2 = (bf16[64,1024]{1,0:T(8,128)(2,1)}, bf16[64,1024]{1,0:T(8,128)(2,1)S(1)}, u32[]{:S(2)}, u32[]{:S(2)}) collective-permute-start(bf16[64,1024]{1,0:T(8,128)(2,1)} %get-tuple-element.19), channel_id=1, source_target_pairs={{0,1},{1,0},{2,3},{3,2},{4,5},{5,4},{6,7},{7,6},{8,9},{9,8},{10,11... | collective-permute-start | bytes 393224 | tf_op jit(solution)/shard_map/ppermute | solution.py:145
  68.1 4.3 %collective-permute-done.2 = bf16[64,1024]{1,0:T(8,128)(2,1)S(1)} collective-permute-done((bf16[64,1024]{1,0:T(8,128)(2,1)}, bf16[64,1024]{1,0:T(8,128)(2,1)S(1)}, u32[]{:S(2)}, u32[]{:S(2)}) %collective-permute-start.2) | collective-permute-done | bytes 131104 | tf_op jit(solution)/shard_map/ppermute | solution.py:145
  72.4 1.0 fusion
  73.4 2.8 %collective-permute-start.3 = (bf16[64,1024]{1,0:T(8,128)(2,1)S(1)}, bf16[64,1024]{1,0:T(8,128)(2,1)S(1)}, u32[]{:S(2)}, u32[]{:S(2)}) collective-permute-start(bf16[64,1024]{1,0:T(8,128)(2,1)S(1)} %fusion), channel_id=1, source_target_pairs={{0,2},{1,3},{2,0},{3,1},{4,6},{5,7},{6,4},{7,5},{8,10},{9,11},{10,... | collective-permute-start | bytes 393224 | tf_op jit(solution)/shard_map/ppermute | solution.py:145
  76.2 6.1 %collective-permute-done.3 = bf16[64,1024]{1,0:T(8,128)(2,1)S(1)} collective-permute-done((bf16[64,1024]{1,0:T(8,128)(2,1)S(1)}, bf16[64,1024]{1,0:T(8,128)(2,1)S(1)}, u32[]{:S(2)}, u32[]{:S(2)}) %collective-permute-start.3) | collective-permute-done | bytes 131104 | tf_op jit(solution)/shard_map/ppermute | solution.py:145
  82.3 1.0 convert_add_fusion.2.pred_ref
  83.3 0.0 copy-start.2
  83.3 1.3 %collective-permute-start.4 = (f32[64,256]{1,0:T(8,128)S(1)}, f32[64,256]{1,0:T(8,128)S(1)}, u32[]{:S(2)}, u32[]{:S(2)}) collective-permute-start(f32[64,256]{1,0:T(8,128)S(1)} %slice.22), channel_id=1, source_target_pairs={{0,4},{4,8},{8,12},{1,5},{5,9},{9,13},{2,6},{6,10},{10,14},{3,7},{... | collective-permute-start | bytes 196616 | tf_op jit(solution)/shard_map/ppermute | solution.py:201
  84.7 0.0 copy-done.3
  84.7 0.6 pad.4.bank_ref
  85.3 0.3 collective-permute-done.4
  85.5 0.6 reverse_select_fusion
  86.2 0.0 copy-done.2
  86.2 3.0 %filter.1.filtered_ref = bf16[64,1024]{1,0:T(8,128)(2,1)} custom-call(s32[4]{0:T(128)} %seg_ref.1, f32[8,512]{1,0:T(8,128)} %pad.4.bank_ref, f32[64,256]{1,0:T(8,128)} %bitcast.7, f32[64,1024]{1,0:T(8,128)} %copy-done.2), custom_call_target="tpu_custom_call" | custom-call | flops 402653184 | bytes 524288 | tf_op jit(solution)/shard_map/filter/pallas_call | solution.py:210
  89.2 10.3 %residual.2 = (f32[32,8192]{1,0:T(8,128)}, bf16[32,8192]{1,0:T(8,128)(2,1)}) custom-call(bf16[64,1024]{1,0:T(8,128)(2,1)} %filter.1.filtered_ref, bf16[1024,8192]{1,0:T(8,128)(2,1)} %get-tuple-element.17.old_ref.design_ref), custom_call_target="tpu_custom_call" | custom-call | flops 1073741824 | bytes 16777216 | tf_op jit(solution)/shard_map/residual/pallas_call | solution.py:221
  99.5 2.7 %collective-permute-start.5 = (bf16[32,8192]{1,0:T(8,128)(2,1)}, bf16[32,8192]{1,0:T(8,128)(2,1)S(1)}, u32[]{:S(2)}, u32[]{:S(2)}) collective-permute-start(bf16[32,8192]{1,0:T(8,128)(2,1)} %get-tuple-element.21), channel_id=1, source_target_pairs={{0,4},{4,0},{8,12},{12,8},{1,5},{5,1},{9,13},{13,9},{2,6},{6,2},{1... | collective-permute-start | bytes 1572872 | tf_op jit(solution)/shard_map/ppermute | solution.py:145
  102.3 0.0 copy-start.1
  102.3 10.4 %residual.3 = (f32[32,8192]{1,0:T(8,128)}, bf16[32,8192]{1,0:T(8,128)(2,1)}) custom-call(bf16[64,1024]{1,0:T(8,128)(2,1)} %filter.1.filtered_ref, bf16[1024,8192]{1,0:T(8,128)(2,1)} %get-tuple-element.22.design_ref), custom_call_target="tpu_custom_call" | custom-call | flops 1073741824 | bytes 16777216 | tf_op jit(solution)/shard_map/residual/pallas_call | solution.py:221
  112.7 0.0 collective-permute-start.7
  112.7 0.0 collective-permute-done.5
  112.7 0.0 copy-done.1
  112.7 0.1 convert_add_fusion.1
  112.9 2.8 %collective-permute-start.6 = (bf16[16,8192]{1,0:T(8,128)(2,1)S(1)}, bf16[16,8192]{1,0:T(8,128)(2,1)S(1)}, u32[]{:S(2)}, u32[]{:S(2)}) collective-permute-start(bf16[16,8192]{1,0:T(8,128)(2,1)S(1)} %slice.32), channel_id=1, source_target_pairs={{0,8},{4,12},{8,0},{12,4},{1,9},{5,13},{9,1},{13,5},{2,10},{6,14},... | collective-permute-start | bytes 786440 | tf_op jit(solution)/shard_map/ppermute | solution.py:145
  115.7 0.0 collective-permute-done.7
  115.7 1.3 %convert_add_fusion = f32[32,8192]{1,0:T(8,128)S(1)} fusion(f32[32,8192]{1,0:T(8,128)} %get-tuple-element.23, bf16[32,8192]{1,0:T(8,128)(2,1)S(1)} %collective-permute-done.7), kind=kLoop, calls=%fused_computation.3 | loop fusion | flops 524288 | bytes 2621440 | tf_op jit(solution)/shard_map/add | solution.py:231
  117.0 1.6 %collective-permute-start.8 = (bf16[16,8192]{1,0:T(8,128)(2,1)S(1)}, bf16[16,8192]{1,0:T(8,128)(2,1)S(1)}, u32[]{:S(2)}, u32[]{:S(2)}) collective-permute-start(bf16[16,8192]{1,0:T(8,128)(2,1)S(1)} %slice.31), channel_id=1, source_target_pairs={{0,8},{4,12},{8,0},{12,4},{1,9},{5,13},{9,1},{13,5},{2,10},{6,14},... | collective-permute-start | bytes 786440 | tf_op jit(solution)/shard_map/ppermute | solution.py:145
  118.6 4.2 %collective-permute-done.6 = bf16[16,8192]{1,0:T(8,128)(2,1)S(1)} collective-permute-done((bf16[16,8192]{1,0:T(8,128)(2,1)S(1)}, bf16[16,8192]{1,0:T(8,128)(2,1)S(1)}, u32[]{:S(2)}, u32[]{:S(2)}) %collective-permute-start.6) | collective-permute-done | bytes 262176 | tf_op jit(solution)/shard_map/ppermute | solution.py:145
  122.9 4.9 %collective-permute-done.8 = bf16[16,8192]{1,0:T(8,128)(2,1)S(1)} collective-permute-done((bf16[16,8192]{1,0:T(8,128)(2,1)S(1)}, bf16[16,8192]{1,0:T(8,128)(2,1)S(1)}, u32[]{:S(2)}, u32[]{:S(2)}) %collective-permute-start.8) | collective-permute-done | bytes 262176 | tf_op jit(solution)/shard_map/ppermute | solution.py:145
  127.8 0.1 slice_add_fusion
  127.8 1.0 pad_maximum_fusion.2
  (5 shorter events, 0.1 us)
Async XLA Ops:
  0.0 15.1 %collective-permute-start = (bf16[16,16384]{1,0:T(8,128)(2,1)}, bf16[16,16384]{1,0:T(8,128)(2,1)S(1)}, u32[]{:S(2)}, u32[]{:S(2)}) collective-permute-start(bf16[16,16384]{1,0:T(8,128)(2,1)} %param.8), channel_id=1, source_target_pairs={{0,8},{4,12},{8,0},{12,4},{1,9},{5,13},{9,1},{13,5},{2,10},{6,14},... | collective-permute-start | bytes 1572872 | tf_op jit(solution)/shard_map/ppermute | solution.py:145
  16.2 19.8 %collective-permute-start.1 = (bf16[32,16384]{1,0:T(8,128)(2,1)S(1)}, bf16[32,16384]{1,0:T(8,128)(2,1)S(1)}, u32[]{:S(2)}, u32[]{:S(2)}) collective-permute-start(bf16[32,16384]{1,0:T(8,128)(2,1)S(1)} %pad_maximum_fusion.1), channel_id=1, source_target_pairs={{0,4},{4,0},{8,12},{12,8},{1,5},{5,1},{9,13},{13,9},{2,6},{6,2},{1... | collective-permute-start | bytes 3145736 | tf_op jit(solution)/shard_map/ppermute | solution.py:145
  16.3 19.8 %copy-start = (bf16[16,16384]{1,0:T(8,128)(2,1)S(1)}, bf16[16,16384]{1,0:T(8,128)(2,1)}, u32[]{:S(2)}) copy-start(bf16[16,16384]{1,0:T(8,128)(2,1)} %param.8) | copy-start | bytes 1572868
  37.5 47.1 %copy-start.3 = (f32[8,255]{1,0:T(8,128)S(1)}, f32[8,255]{1,0:T(8,128)}, u32[]{:S(2)}) copy-start(f32[8,255]{1,0:T(8,128)} %param.14) | copy-start | bytes 24484
  66.2 6.2 %collective-permute-start.2 = (bf16[64,1024]{1,0:T(8,128)(2,1)}, bf16[64,1024]{1,0:T(8,128)(2,1)S(1)}, u32[]{:S(2)}, u32[]{:S(2)}) collective-permute-start(bf16[64,1024]{1,0:T(8,128)(2,1)} %get-tuple-element.19), channel_id=1, source_target_pairs={{0,1},{1,0},{2,3},{3,2},{4,5},{5,4},{6,7},{7,6},{8,9},{9,8},{10,11... | collective-permute-start | bytes 393224 | tf_op jit(solution)/shard_map/ppermute | solution.py:145
  73.4 8.9 %collective-permute-start.3 = (bf16[64,1024]{1,0:T(8,128)(2,1)S(1)}, bf16[64,1024]{1,0:T(8,128)(2,1)S(1)}, u32[]{:S(2)}, u32[]{:S(2)}) collective-permute-start(bf16[64,1024]{1,0:T(8,128)(2,1)S(1)} %fusion), channel_id=1, source_target_pairs={{0,2},{1,3},{2,0},{3,1},{4,6},{5,7},{6,4},{7,5},{8,10},{9,11},{10,... | collective-permute-start | bytes 393224 | tf_op jit(solution)/shard_map/ppermute | solution.py:145
  83.3 2.8 %copy-start.2 = (f32[64,1024]{1,0:T(8,128)}, f32[64,1024]{1,0:T(8,128)S(1)}, u32[]{:S(2)}) copy-start(f32[64,1024]{1,0:T(8,128)S(1)} %convert_add_fusion.2.pred_ref) | copy-start | bytes 786436
  83.3 2.2 %collective-permute-start.4 = (f32[64,256]{1,0:T(8,128)S(1)}, f32[64,256]{1,0:T(8,128)S(1)}, u32[]{:S(2)}, u32[]{:S(2)}) collective-permute-start(f32[64,256]{1,0:T(8,128)S(1)} %slice.22), channel_id=1, source_target_pairs={{0,4},{4,8},{8,12},{1,5},{5,9},{9,13},{2,6},{6,10},{10,14},{3,7},{... | collective-permute-start | bytes 196616 | tf_op jit(solution)/shard_map/ppermute | solution.py:201
  99.5 13.2 %collective-permute-start.5 = (bf16[32,8192]{1,0:T(8,128)(2,1)}, bf16[32,8192]{1,0:T(8,128)(2,1)S(1)}, u32[]{:S(2)}, u32[]{:S(2)}) collective-permute-start(bf16[32,8192]{1,0:T(8,128)(2,1)} %get-tuple-element.21), channel_id=1, source_target_pairs={{0,4},{4,0},{8,12},{12,8},{1,5},{5,1},{9,13},{13,9},{2,6},{6,2},{1... | collective-permute-start | bytes 1572872 | tf_op jit(solution)/shard_map/ppermute | solution.py:145
  102.3 10.4 %copy-start.1 = (f32[32,8192]{1,0:T(8,128)S(1)}, f32[32,8192]{1,0:T(8,128)}, u32[]{:S(2)}) copy-start(f32[32,8192]{1,0:T(8,128)} %get-tuple-element.20) | copy-start | bytes 3145732
  112.7 3.0 %collective-permute-start.7 = (bf16[32,8192]{1,0:T(8,128)(2,1)}, bf16[32,8192]{1,0:T(8,128)(2,1)S(1)}, u32[]{:S(2)}, u32[]{:S(2)}) collective-permute-start(bf16[32,8192]{1,0:T(8,128)(2,1)} %get-tuple-element.24), channel_id=1, source_target_pairs={{0,4},{4,0},{8,12},{12,8},{1,5},{5,1},{9,13},{13,9},{2,6},{6,2},{1... | collective-permute-start | bytes 1572872 | tf_op jit(solution)/shard_map/ppermute | solution.py:145
  112.9 10.0 %collective-permute-start.6 = (bf16[16,8192]{1,0:T(8,128)(2,1)S(1)}, bf16[16,8192]{1,0:T(8,128)(2,1)S(1)}, u32[]{:S(2)}, u32[]{:S(2)}) collective-permute-start(bf16[16,8192]{1,0:T(8,128)(2,1)S(1)} %slice.32), channel_id=1, source_target_pairs={{0,8},{4,12},{8,0},{12,4},{1,9},{5,13},{9,1},{13,5},{2,10},{6,14},... | collective-permute-start | bytes 786440 | tf_op jit(solution)/shard_map/ppermute | solution.py:145
  117.0 10.7 %collective-permute-start.8 = (bf16[16,8192]{1,0:T(8,128)(2,1)S(1)}, bf16[16,8192]{1,0:T(8,128)(2,1)S(1)}, u32[]{:S(2)}, u32[]{:S(2)}) collective-permute-start(bf16[16,8192]{1,0:T(8,128)(2,1)S(1)} %slice.31), channel_id=1, source_target_pairs={{0,8},{4,12},{8,0},{12,4},{1,9},{5,13},{9,1},{13,5},{2,10},{6,14},... | collective-permute-start | bytes 786440 | tf_op jit(solution)/shard_map/ppermute | solution.py:145

commit v2 on v1

--- a/solution.py
+++ b/solution.py
@@ -7,10 +7,13 @@
 from jax.experimental.pallas import tpu as pltpu
 from jax.sharding import PartitionSpec as P
 
+
 SEG = 256
 ORDERS = 256
 ROWS = 256
 COLS = 1024
+KERNEL_VMEM = 10 << 20
+SMALL_VMEM = 6 << 20
 INV_TWO_PI = 0.15915494309189535
 TWO_PI_HI = 6.28125
 TWO_PI_LO = 0.0019353071795864769
@@ -59,7 +62,7 @@
         trig_ref[rows, ORDERS:] = (rest * horner(SIN, square)).astype(BF16)
 
 
-def design_tile(weights_ref, trig_ref, code_ref, legendre_ref, rows, chosen):
+def design_tile(weights_ref, trig_ref, legendre_ref, rows, chosen):
     interp = dot(weights_ref[rows, :], legendre_ref[...])
     phases = dot(trig_ref[rows, :], chosen)
     return (interp * phases).astype(BF16)
@@ -77,26 +80,30 @@
     def _():
         fill_tables(bin_ref, frac_ref, lon_ref, weights_ref, trig_ref)
 
+    step = pl.program_id(0)
     chosen = one_hot(code_ref)
-    for first in range(0, design_ref.shape[0], ROWS):
+    for first in range(0, design_ref.shape[1], ROWS):
         rows = slice(first, first + ROWS)
-        design_ref[rows, :] = design_tile(weights_ref, trig_ref, code_ref, legendre_ref, rows, chosen)
-
-
-def second_kernel(weights_ref, trig_ref, code_ref, legendre_ref, probes_ref, old_ref, old_probes_ref,
-                  design_ref, pred_ref, sent_ref, total_ref):
+        design_ref[step, rows, :] = design_tile(weights_ref, trig_ref, legendre_ref, rows, chosen)
+
+
+def second_kernel(blocks, weights_ref, trig_ref, code_ref, legendre_ref, old_ref, *refs):
+    probe_refs, old_probe_refs = refs[:blocks], refs[blocks : 2 * blocks]
+    design_ref, pred_ref, sent_ref, total_ref = refs[2 * blocks :]
     step = pl.program_id(0)
 
     @pl.when(step == 0)
     def _():
         total_ref[...] = jnp.zeros_like(total_ref)
 
+    probes = jnp.concatenate([ref[...] for ref in probe_refs], axis=0)
+    old_probes = jnp.concatenate([ref[...] for ref in old_probe_refs], axis=0)
     chosen = one_hot(code_ref)
-    for first in range(0, design_ref.shape[0], ROWS):
+    for first in range(0, design_ref.shape[1], ROWS):
         rows = slice(first, first + ROWS)
-        tile = design_tile(weights_ref, trig_ref, code_ref, legendre_ref, rows, chosen)
-        design_ref[rows, :] = tile
-        total_ref[rows, :] += dot_t(tile, probes_ref[...]) + dot_t(old_ref[rows, :], old_probes_ref[...])
+        tile = design_tile(weights_ref, trig_ref, legendre_ref, rows, chosen)
+        design_ref[step, rows, :] = tile
+        total_ref[rows, :] += dot_t(tile, probes) + dot_t(old_ref[step, rows, :], old_probes)
 
     @pl.when(step == pl.num_programs(0) - 1)
     def _():
@@ -105,20 +112,41 @@
         sent_ref[...] = total.astype(BF16)
 
 
-def filter_kernel(seg_ref, bank_ref, before_ref, pred_ref, out_ref):
-    for segment in range(pred_ref.shape[1] // SEG):
+def tables_kernel(seg_ref, bank_ref, high_ref, low_ref):
+    for segment in range(high_ref.shape[0]):
         taps = bank_ref[pl.ds(seg_ref[segment], 1), :]
         spread = jnp.broadcast_to(taps, (2 * SEG, 2 * SEG))
         table = pltpu.roll(spread, SEG, 1, stride=1, stride_axis=0)[:, :SEG]
+        high = table.astype(BF16)
+        high_ref[segment] = high
+        low_ref[segment] = (table - high.astype(F32)).astype(BF16)
+
+
+def filter_kernel(bits, before_ref, pred_ref, high_ref, low_ref, out_ref):
+    before = before_ref[...]
+    count = before.shape[0]
+    here = lax.axis_index("epoch")
+    differing = here ^ (here - 1)
+    place = lax.broadcasted_iota(jnp.int32, before.shape, 0)
+    stride = count
+    for bit in bits:
+        stride //= 2
+        up, down = pltpu.roll(before, stride, 0), pltpu.roll(before, count - stride, 0)
+        flipped = jnp.where((place & stride) != 0, up, down)
+        before = jnp.where((differing & bit) != 0, flipped, before)
+
+    for segment in range(pred_ref.shape[1] // SEG):
         here = pred_ref[:, segment * SEG : (segment + 1) * SEG]
-        past = before_ref[...] if segment == 0 else pred_ref[:, (segment - 1) * SEG : segment * SEG]
+        past = before if segment == 0 else pred_ref[:, (segment - 1) * SEG : segment * SEG]
         window = jnp.concatenate([past, here], axis=1)
-        value = jnp.dot(window, table, precision=lax.Precision.HIGHEST, preferred_element_type=F32)
+        high = window.astype(BF16)
+        low = (window - high.astype(F32)).astype(BF16)
+        value = dot(high, high_ref[segment]) + (dot(high, low_ref[segment]) + dot(low, high_ref[segment]))
         out_ref[:, segment * SEG : (segment + 1) * SEG] = value.astype(BF16)
 
 
 def residual_kernel(filtered_ref, design_ref, kept_ref, sent_ref):
-    value = dot(filtered_ref[...], design_ref[...])
+    value = dot(filtered_ref[...], design_ref[pl.program_id(0)])
     half = kept_ref.shape[0]
     kept_ref[...] = value[:half]
     sent_ref[...] = value[half:].astype(BF16)
@@ -134,6 +162,10 @@
 
 def across(rows, cols, shift=0):
     return pl.BlockSpec((rows, cols), lambda c: (0, c + shift))
+
+
+def resident(array):
+    return pltpu.with_memory_space_constraint(array, pltpu.VMEM)
 
 
 def cost(flops, nbytes):
@@ -155,43 +187,72 @@
     epoch_bits = bits_of("epoch")
     row = lambda array: array.reshape(1, -1)
     codes = row(order_code)
+    legendre = pltpu.with_memory_space_constraint(legendre, pltpu.HBM)
     half = coeffs // 2
     cols = min(COLS, half)
     steps = half // cols
 
-    gathered = probes
-    for bit in reversed(epoch_bits):
-        gathered = jnp.concatenate([gathered, swapped(gathered, "epoch", bit)], axis=0)
-    count = gathered.shape[0]
+    vmem, smem = pl.BlockSpec(memory_space=pltpu.VMEM), pl.BlockSpec(memory_space=pltpu.SMEM)
+    taps = jnp.pad(bank, ((0, 0), (0, 2 * SEG - bank.shape[1])))
+    segments = epochs // SEG
+    high, low = pl.pallas_call(
+        tables_kernel,
+        in_specs=[smem, vmem],
+        out_specs=[vmem] * 2,
+        out_shape=[struct((segments, 2 * SEG, SEG), BF16)] * 2,
+        cost_estimate=cost(40 * segments * SEG * SEG, 8 * segments * SEG * SEG),
+        compiler_params=pltpu.CompilerParams(vmem_limit_bytes=SMALL_VMEM),
+        name="tables",
+    )(seg_filter, taps)
+
+    blocks = [probes]
+    for bit in reversed(epoch_bits[1:]):
+        blocks += [swapped(block, "epoch", bit) for block in blocks]
 
     design_1, weights, trig = pl.pallas_call(
         first_kernel,
         grid=(steps,),
         in_specs=[whole((1, epochs))] * 3 + [across(1, cols), across(nodes, cols)],
-        out_specs=[across(epochs, cols), whole((epochs, nodes)), whole((epochs, 2 * ORDERS))],
-        out_shape=[struct((epochs, half), BF16), struct((epochs, nodes), BF16), struct((epochs, 2 * ORDERS), BF16)],
+        out_specs=[vmem, whole((epochs, nodes)), whole((epochs, 2 * ORDERS))],
+        out_shape=[
+            pltpu.VMEM((steps, epochs, cols), BF16),
+            struct((epochs, nodes), BF16),
+            struct((epochs, 2 * ORDERS), BF16),
+        ],
         cost_estimate=cost(2 * epochs * half * (nodes + 2 * ORDERS), 2 * half * (epochs + nodes)),
+        compiler_params=pltpu.CompilerParams(vmem_limit_bytes=KERNEL_VMEM),
         name="design_first",
     )(row(lat_bin), row(lat_frac), row(longitude), codes, legendre)
+    blocks, design_1 = lax.optimization_barrier((blocks, design_1))
+    blocks = blocks + [swapped(block, "epoch", epoch_bits[0]) for block in blocks]
+    count = own * len(blocks)
+    if own % 16:
+        blocks = [jnp.concatenate(blocks, axis=0)]
+    height = blocks[0].shape[0]
 
     design_2, pred, sent = pl.pallas_call(
-        second_kernel,
+        functools.partial(second_kernel, len(blocks)),
         grid=(steps,),
         in_specs=[
             whole((epochs, nodes)),
             whole((epochs, 2 * ORDERS)),
             across(1, cols, steps),
             across(nodes, cols, steps),
-            across(count, cols, steps),
-            across(epochs, cols),
-            across(count, cols),
+            vmem,
+        ]
+        + [across(height, cols, steps)] * len(blocks)
+        + [across(height, cols)] * len(blocks),
+        out_specs=[vmem, whole((count, epochs)), whole((count, epochs))],
+        out_shape=[
+            pltpu.VMEM((steps, epochs, cols), BF16),
+            struct((count, epochs), F32),
+            struct((count, epochs), BF16),
         ],
-        out_specs=[across(epochs, cols), whole((count, epochs)), whole((count, epochs))],
-        out_shape=[struct((epochs, half), BF16), struct((count, epochs), F32), struct((count, epochs), BF16)],
         scratch_shapes=[pltpu.VMEM((epochs, count), F32)],
         cost_estimate=cost(2 * epochs * half * (nodes + 2 * ORDERS + 2 * count), 2 * half * (2 * epochs + nodes)),
+        compiler_params=pltpu.CompilerParams(vmem_limit_bytes=KERNEL_VMEM),
         name="design_second",
-    )(weights, trig, codes, legendre, gathered, design_1, gathered)
+    )(weights, trig, codes, legendre, resident(design_1), *blocks, *blocks)
 
     for bit in bits_of("param"):
         pred = pred + swapped(sent, "param", bit).astype(F32)
@@ -199,39 +260,35 @@
 
     devices = lax.axis_size("epoch")
     before = lax.ppermute(pred[:, epochs - SEG :], "epoch", [(i, i + 1) for i in range(devices - 1)])
-    here = lax.axis_index("epoch")
-    differing = here ^ (here - 1)
-    before = before.reshape((2,) * len(epoch_bits) + (own, SEG))
-    for place, bit in enumerate(epoch_bits):
-        before = jnp.where((differing & bit) != 0, jnp.flip(before, place), before)
-    before = before.reshape(count, SEG)
-
-    taps = jnp.pad(bank, ((0, 0), (0, 2 * SEG - bank.shape[1])))
     filtered = pl.pallas_call(
-        filter_kernel,
-        in_specs=[pl.BlockSpec(memory_space=pltpu.SMEM)] + [pl.BlockSpec(memory_space=pltpu.VMEM)] * 3,
-        out_specs=pl.BlockSpec(memory_space=pltpu.VMEM),
+        functools.partial(filter_kernel, epoch_bits),
+        in_specs=[vmem] * 4,
+        out_specs=vmem,
         out_shape=struct((count, epochs), BF16),
-        cost_estimate=cost(12 * count * epochs * 2 * SEG, 8 * count * epochs),
+        cost_estimate=cost(6 * count * epochs * 2 * SEG, 8 * count * epochs),
+        compiler_params=pltpu.CompilerParams(vmem_limit_bytes=SMALL_VMEM),
         name="filter",
-    )(seg_filter, taps, before, pred)
+    )(before, pred, high, low)
 
     pieces = []
     for design in (design_1, design_2):
         kept, sent = pl.pallas_call(
             residual_kernel,
             grid=(steps,),
-            in_specs=[whole((count, epochs)), across(epochs, cols)],
+            in_specs=[whole((count, epochs)), vmem],
             out_specs=[across(count // 2, cols)] * 2,
             out_shape=[struct((count // 2, half), F32), struct((count // 2, half), BF16)],
-            cost_estimate=cost(2 * count * epochs * half, 2 * epochs * half),
+            cost_estimate=cost(2 * count * epochs * half, 6 * count * half),
+            compiler_params=pltpu.CompilerParams(vmem_limit_bytes=SMALL_VMEM),
             name="residual",
-        )(filtered, design)
+        )(filtered, resident(design))
         for bit in epoch_bits[:-1]:
             total = kept + swapped(sent, "epoch", bit).astype(F32)
             rows = total.shape[0] // 2
             kept, sent = total[:rows], total[rows:].astype(BF16)
-        pieces.append(kept + swapped(sent, "epoch", epoch_bits[-1]).astype(F32))
+        filtered, sent = lax.optimization_barrier((filtered, sent))
+        received = swapped(sent, "epoch", epoch_bits[-1])
+        pieces.append(kept + received.astype(F32))
     return jnp.concatenate(pieces, axis=1)
 
 

time: 129 us -> 97.7 us (0.76)
  Pallas kernels: 72.2 us -> 53.3 us
  waiting for transfers between devices: 31.9 us -> 23.9 us
  other arithmetic: 7.73 us -> 1.39 us
  local copies, waits for them, and re-layouts: 0.69 us -> 2.98 us
    pallas_call x2, Pallas kernels: 20.8 us -> 8.01 us  [local(): pl.pallas_call(residual_kernel, grid=(steps,), in_specs=[whole((count, ep...]
    ppermute x8 -> x9, waiting for transfers between devices: 31.7 us -> 23.9 us  [swapped(): return lax.ppermute(array, axis, [(i, i ^ bit) for i in range(size)])]
    pallas_call x2 -> x3, Pallas kernels: 31.7 us -> 26.9 us  [the longest x1 25.4 us: local(): pl.pallas_call(functools.partial(second_kernel, len(blocks)), grid=(steps...]
    unnamed x8 -> x14, local copies, waits for them, and re-layouts: 0.02 us -> 2.91 us
    concatenate x2 -> x0, other arithmetic: 2.57 us -> none  [local(): jnp.concatenate([gathered, swapped(gathered, 'epoch', bit)], axis=0)]
    pallas_call x1, Pallas kernels: 19.7 us -> 18.4 us  [local(): pl.pallas_call(first_kernel, grid=(steps,), in_specs=[whole((1, epochs))]...]
    ppermute x8 -> x9, starting transfers between devices: 14.9 us -> 14.3 us  [swapped(): return lax.ppermute(array, axis, [(i, i ^ bit) for i in range(size)])]
  transfers between devices with their start and end apart: 9 -> 10, of which waited for: 6 -> 7; matrix products, arithmetic and copies ran while one was open for 2% -> 0% of each run, Pallas kernels for 23% -> 20%
where the time goes in v2:
time: 97.7 us; the launch traced here: 97.4 us
  Pallas kernels  53.3 us (55%)
  waiting for transfers between devices  23.9 us (24%)
  starting transfers between devices  15.6 us (16%)
  local copies, waits for them, and re-layouts  2.98 us (3%)
  other arithmetic  1.39 us (1%)
    pallas_call x1, Pallas kernels, local(): pl.pallas_call(functools.partial(second_kernel, len(blocks)), grid=(steps...  25.4 us
    ppermute x9, waiting for transfers between devices, swapped(): return lax.ppermute(array, axis, [(i, i ^ bit) for i in range(size)])  23.9 us
    pallas_call x1, Pallas kernels, local(): pl.pallas_call(first_kernel, grid=(steps,), in_specs=[whole((1, epochs))]...  18.4 us
    ppermute x9, starting transfers between devices, swapped(): return lax.ppermute(array, axis, [(i, i ^ bit) for i in range(size)])  14.3 us
    pallas_call x2, Pallas kernels, local(): pl.pallas_call(residual_kernel, grid=(steps,), in_specs=[whole((count, ep...  8.01 us
    unnamed x14, local copies, waits for them, and re-layouts  2.91 us
  transfers between devices with their start and end apart: 10, of which 7 were waited for; matrix products, arithmetic and copies ran while one was open for 0% of the time, Pallas kernels for 20%

profile of v2, /device:TPU:0, one launch (start us, length us, event | category | flops | bytes accessed | tf_op | source)
XLA Modules:
  0.0 97.4 jit_solution(13715537959313206473)
XLA Ops:
  0.0 3.0 %collective-permute-start = (bf16[16,16384]{1,0:T(8,128)(2,1)}, bf16[16,16384]{1,0:T(8,128)(2,1)S(1)}, u32[]{:S(2)}, u32[]{:S(2)}) collective-permute-start(bf16[16,16384]{1,0:T(8,128)(2,1)} %refs_4_), channel_id=1, source_target_pairs={{0,8},{4,12},{8,0},{12,4},{1,9},{5,13},{9,1},{13,5},{2,10},{6,14},... | collective-permute-start | bytes 1572872 | tf_op jit(solution)/shard_map/ppermute | solution.py:177
  3.0 0.0 copy-start.1
  3.0 0.8 copy-done.1
  3.8 0.0 copy-start.2
  3.8 0.7 copy-done.2
  4.5 0.0 copy-start.3
  4.5 0.7 copy-done.3
  5.2 0.0 copy-start.4
  5.2 0.7 copy-done.4
  5.9 0.0 copy-start
  5.9 18.4 %design_first.1 = (bf16[8,1024,1024]{2,1,0:T(8,128)(2,1)S(1)}, bf16[1024,256]{1,0:T(8,128)(2,1)S(1)}, bf16[1024,512]{1,0:T(8,128)(2,1)S(1)}) custom-call(s32[1,1024]{1,0:T(1,128)S(1)} %bitcast.6, f32[1,1024]{1,0:T(1,128)S(1)} %bitcast.7, f32[1,1024]{1,0:T(1,128)S(1)} %bitcast.8, s32[1,16384]{1,0:T(1,128)S(1)} %bitcast.4, bf16[256,16384]{1,0:T(8,128)(2,1)} %legendre_ref.3), custom_call_target="tpu_custom_call" | custom-call | flops 12884901888 | bytes 20971520 | tf_op jit(solution)/shard_map/design_first/pallas_call | solution.py:212
  24.3 0.0 collective-permute-done.refs_1_.refs_5_
  24.3 0.0 copy-done
  24.3 0.1 collective-permute-start.1
  24.4 0.5 collective-permute-start.2
  24.9 1.4 %collective-permute-done.1.refs_2_.refs_6_ = bf16[16,16384]{1,0:T(8,128)(2,1)S(1)} collective-permute-done((bf16[16,16384]{1,0:T(8,128)(2,1)S(1)}, bf16[16,16384]{1,0:T(8,128)(2,1)S(1)}, u32[]{:S(2)}, u32[]{:S(2)}) %collective-permute-start.1) | collective-permute-done | bytes 524320 | tf_op jit(solution)/shard_map/ppermute | solution.py:177
  26.3 0.7 collective-permute-done.2.refs_3_.refs_7_
  27.1 0.0 copy-start.6
  27.1 0.0 copy-start.5
  27.1 25.4 %design_second.1 = (bf16[8,1024,1024]{2,1,0:T(8,128)(2,1)S(1)}, f32[64,1024]{1,0:T(8,128)S(1)}, bf16[64,1024]{1,0:T(8,128)(2,1)S(1)}) custom-call(bf16[1024,256]{1,0:T(8,128)(2,1)S(1)} %get-tuple-element.23.weights_ref, bf16[1024,512]{1,0:T(8,128)(2,1)S(1)} %get-tuple-element.24.trig_ref, s32[1,16384]{1,0:T(1,128)S(1)} %bitcast.5, ...), custom_call_target="tpu_custom_call" | custom-call | flops 15032385536 | bytes 37748736 | tf_op jit(solution)/shard_map/design_second/pallas_call | solution.py:233
  52.4 1.6 %collective-permute-start.3 = (bf16[64,1024]{1,0:T(8,128)(2,1)S(1)}, bf16[64,1024]{1,0:T(8,128)(2,1)S(1)}, u32[]{:S(2)}, u32[]{:S(2)}) collective-permute-start(bf16[64,1024]{1,0:T(8,128)(2,1)S(1)} %get-tuple-element.30), channel_id=1, source_target_pairs={{0,1},{1,0},{2,3},{3,2},{4,5},{5,4},{6,7},{7,6},{8,9},{9,8},{10,11... | collective-permute-start | bytes 393224 | tf_op jit(solution)/shard_map/ppermute | solution.py:177
  54.1 4.0 %collective-permute-done.3 = bf16[64,1024]{1,0:T(8,128)(2,1)S(1)} collective-permute-done((bf16[64,1024]{1,0:T(8,128)(2,1)S(1)}, bf16[64,1024]{1,0:T(8,128)(2,1)S(1)}, u32[]{:S(2)}, u32[]{:S(2)}) %collective-permute-start.3) | collective-permute-done | bytes 131104 | tf_op jit(solution)/shard_map/ppermute | solution.py:177
  58.1 2.7 %collective-permute-start.4 = (bf16[64,1024]{1,0:T(8,128)(2,1)S(1)}, bf16[64,1024]{1,0:T(8,128)(2,1)S(1)}, u32[]{:S(2)}, u32[]{:S(2)}) collective-permute-start(bf16[64,1024]{1,0:T(8,128)(2,1)S(1)} %fusion), channel_id=1, source_target_pairs={{0,2},{1,3},{2,0},{3,1},{4,6},{5,7},{6,4},{7,5},{8,10},{9,11},{10,... | collective-permute-start | bytes 393224 | tf_op jit(solution)/shard_map/ppermute | solution.py:177
  60.7 5.8 %collective-permute-done.4 = bf16[64,1024]{1,0:T(8,128)(2,1)S(1)} collective-permute-done((bf16[64,1024]{1,0:T(8,128)(2,1)S(1)}, bf16[64,1024]{1,0:T(8,128)(2,1)S(1)}, u32[]{:S(2)}, u32[]{:S(2)}) %collective-permute-start.4) | collective-permute-done | bytes 131104 | tf_op jit(solution)/shard_map/ppermute | solution.py:177
  66.6 1.3 %collective-permute-start.5 = (f32[64,256]{1,0:T(8,128)S(1)}, f32[64,256]{1,0:T(8,128)S(1)}, u32[]{:S(2)}, u32[]{:S(2)}) collective-permute-start(f32[64,256]{1,0:T(8,128)S(1)} %slice.22), channel_id=1, source_target_pairs={{0,4},{4,8},{8,12},{1,5},{5,9},{9,13},{2,6},{6,10},{10,14},{3,7},{... | collective-permute-start | bytes 196616 | tf_op jit(solution)/shard_map/ppermute | solution.py:262
  67.9 0.0 copy-done.6
  67.9 0.0 copy-done.5
  67.9 0.9 tables.1
  68.8 0.0 collective-permute-done.5.before_ref
  68.8 0.7 filter.1.filtered_ref
  69.5 4.0 %residual.2 = (f32[32,8192]{1,0:T(8,128)S(1)}, bf16[32,8192]{1,0:T(8,128)(2,1)S(1)}) custom-call(bf16[64,1024]{1,0:T(8,128)(2,1)S(1)} %filter.1.filtered_ref, bf16[8,1024,1024]{2,1,0:T(8,128)(2,1)S(1)} %get-tuple-element.26.old_ref.design_ref), custom_call_target="tpu_custom_call" | custom-call | flops 1073741824 | bytes 3145728 | tf_op jit(solution)/shard_map/residual/pallas_call | solution.py:275
  73.5 1.8 %collective-permute-start.6 = (bf16[32,8192]{1,0:T(8,128)(2,1)S(1)}, bf16[32,8192]{1,0:T(8,128)(2,1)S(1)}, u32[]{:S(2)}, u32[]{:S(2)}) collective-permute-start(bf16[32,8192]{1,0:T(8,128)(2,1)S(1)} %get-tuple-element.34), channel_id=1, source_target_pairs={{0,4},{4,0},{8,12},{12,8},{1,5},{5,1},{9,13},{13,9},{2,6},{6,2},{1... | collective-permute-start | bytes 1572872 | tf_op jit(solution)/shard_map/ppermute | solution.py:177
  75.3 1.5 %collective-permute-done.6 = bf16[32,8192]{1,0:T(8,128)(2,1)S(1)} collective-permute-done((bf16[32,8192]{1,0:T(8,128)(2,1)S(1)}, bf16[32,8192]{1,0:T(8,128)(2,1)S(1)}, u32[]{:S(2)}, u32[]{:S(2)}) %collective-permute-start.6) | collective-permute-done | bytes 524320 | tf_op jit(solution)/shard_map/ppermute | solution.py:177
  76.8 0.1 convert_add_fusion.1
  77.0 4.0 %residual.3 = (f32[32,8192]{1,0:T(8,128)S(1)}, bf16[32,8192]{1,0:T(8,128)(2,1)S(1)}) custom-call(bf16[64,1024]{1,0:T(8,128)(2,1)S(1)} %filter.1.filtered_ref, bf16[8,1024,1024]{2,1,0:T(8,128)(2,1)S(1)} %get-tuple-element.37.design_ref), custom_call_target="tpu_custom_call" | custom-call | flops 1073741824 | bytes 3145728 | tf_op jit(solution)/shard_map/residual/pallas_call | solution.py:275
  81.0 0.4 collective-permute-start.8
  81.4 2.4 %collective-permute-start.7 = (bf16[16,8192]{1,0:T(8,128)(2,1)S(1)}, bf16[16,8192]{1,0:T(8,128)(2,1)S(1)}, u32[]{:S(2)}, u32[]{:S(2)}) collective-permute-start(bf16[16,8192]{1,0:T(8,128)(2,1)S(1)} %slice.32), channel_id=1, source_target_pairs={{0,8},{4,12},{8,0},{12,4},{1,9},{5,13},{9,1},{13,5},{2,10},{6,14},... | collective-permute-start | bytes 786440 | tf_op jit(solution)/shard_map/ppermute | solution.py:177
  83.8 0.0 collective-permute-done.8
  83.8 0.1 convert_add_fusion
  83.9 1.8 %collective-permute-start.9 = (bf16[16,8192]{1,0:T(8,128)(2,1)S(1)}, bf16[16,8192]{1,0:T(8,128)(2,1)S(1)}, u32[]{:S(2)}, u32[]{:S(2)}) collective-permute-start(bf16[16,8192]{1,0:T(8,128)(2,1)S(1)} %slice.31), channel_id=1, source_target_pairs={{0,8},{4,12},{8,0},{12,4},{1,9},{5,13},{9,1},{13,5},{2,10},{6,14},... | collective-permute-start | bytes 786440 | tf_op jit(solution)/shard_map/ppermute | solution.py:177
  85.8 5.2 %collective-permute-done.7 = bf16[16,8192]{1,0:T(8,128)(2,1)S(1)} collective-permute-done((bf16[16,8192]{1,0:T(8,128)(2,1)S(1)}, bf16[16,8192]{1,0:T(8,128)(2,1)S(1)}, u32[]{:S(2)}, u32[]{:S(2)}) %collective-permute-start.7) | collective-permute-done | bytes 262176 | tf_op jit(solution)/shard_map/ppermute | solution.py:177
  91.0 5.3 %collective-permute-done.9 = bf16[16,8192]{1,0:T(8,128)(2,1)S(1)} collective-permute-done((bf16[16,8192]{1,0:T(8,128)(2,1)S(1)}, bf16[16,8192]{1,0:T(8,128)(2,1)S(1)}, u32[]{:S(2)}, u32[]{:S(2)}) %collective-permute-start.9) | collective-permute-done | bytes 262176 | tf_op jit(solution)/shard_map/ppermute | solution.py:177
  96.2 0.1 slice_add_fusion
  96.3 1.0 %pad_maximum_fusion = f32[16,16384]{1,0:T(8,128)} fusion(f32[16,8192]{1,0:T(8,128)S(1)} %slice_add_fusion, f32[16,8192]{1,0:T(8,128)S(1)} %slice_add_fusion.1), kind=kLoop, calls=%fused_computation | loop fusion | flops 262144 | bytes 2097152 | tf_op jit(solution)/shard_map/concatenate | solution.py:292
  (7 shorter events, 0.2 us)
Async XLA Ops:
  0.0 24.3 %collective-permute-start = (bf16[16,16384]{1,0:T(8,128)(2,1)}, bf16[16,16384]{1,0:T(8,128)(2,1)S(1)}, u32[]{:S(2)}, u32[]{:S(2)}) collective-permute-start(bf16[16,16384]{1,0:T(8,128)(2,1)} %refs_4_), channel_id=1, source_target_pairs={{0,8},{4,12},{8,0},{12,4},{1,9},{5,13},{9,1},{13,5},{2,10},{6,14},... | collective-permute-start | bytes 1572872 | tf_op jit(solution)/shard_map/ppermute | solution.py:177
  3.0 0.8 copy-start.1
  3.8 0.7 copy-start.2
  4.5 0.7 copy-start.3
  5.2 0.7 copy-start.4
  5.9 18.4 %copy-start = (bf16[16,16384]{1,0:T(8,128)(2,1)S(1)}, bf16[16,16384]{1,0:T(8,128)(2,1)}, u32[]{:S(2)}) copy-start(bf16[16,16384]{1,0:T(8,128)(2,1)} %refs_4_) | copy-start | bytes 1572868
  24.3 2.0 %collective-permute-start.1 = (bf16[16,16384]{1,0:T(8,128)(2,1)S(1)}, bf16[16,16384]{1,0:T(8,128)(2,1)S(1)}, u32[]{:S(2)}, u32[]{:S(2)}) collective-permute-start(bf16[16,16384]{1,0:T(8,128)(2,1)S(1)} %copy-done), channel_id=1, source_target_pairs={{0,4},{4,0},{8,12},{12,8},{1,5},{5,1},{9,13},{13,9},{2,6},{6,2},{1... | collective-permute-start | bytes 1572872 | tf_op jit(solution)/shard_map/ppermute | solution.py:177
  24.4 2.6 %collective-permute-start.2 = (bf16[16,16384]{1,0:T(8,128)(2,1)S(1)}, bf16[16,16384]{1,0:T(8,128)(2,1)S(1)}, u32[]{:S(2)}, u32[]{:S(2)}) collective-permute-start(bf16[16,16384]{1,0:T(8,128)(2,1)S(1)} %collective-permute-done.refs_1_.refs_5_), channel_id=1, source_target_pairs={{0,4},{4,0},{8,12},{12,8},{1,5},{5,1},{9,13},{13,9},{2,6},{6,2},{1... | collective-permute-start | bytes 1572872 | tf_op jit(solution)/shard_map/ppermute | solution.py:177
  27.1 40.8 %copy-start.6 = (f32[8,255]{1,0:T(8,128)S(1)}, f32[8,255]{1,0:T(8,128)}, u32[]{:S(2)}) copy-start(f32[8,255]{1,0:T(8,128)} %param.14) | copy-start | bytes 24484
  27.1 40.9 %copy-start.5 = (s32[4]{0:T(128)S(1)}, s32[4]{0:T(128)}, u32[]{:S(2)}) copy-start(s32[4]{0:T(128)} %seg_ref.1) | copy-start | bytes 52
  52.4 5.6 %collective-permute-start.3 = (bf16[64,1024]{1,0:T(8,128)(2,1)S(1)}, bf16[64,1024]{1,0:T(8,128)(2,1)S(1)}, u32[]{:S(2)}, u32[]{:S(2)}) collective-permute-start(bf16[64,1024]{1,0:T(8,128)(2,1)S(1)} %get-tuple-element.30), channel_id=1, source_target_pairs={{0,1},{1,0},{2,3},{3,2},{4,5},{5,4},{6,7},{7,6},{8,9},{9,8},{10,11... | collective-permute-start | bytes 393224 | tf_op jit(solution)/shard_map/ppermute | solution.py:177
  58.1 8.5 %collective-permute-start.4 = (bf16[64,1024]{1,0:T(8,128)(2,1)S(1)}, bf16[64,1024]{1,0:T(8,128)(2,1)S(1)}, u32[]{:S(2)}, u32[]{:S(2)}) collective-permute-start(bf16[64,1024]{1,0:T(8,128)(2,1)S(1)} %fusion), channel_id=1, source_target_pairs={{0,2},{1,3},{2,0},{3,1},{4,6},{5,7},{6,4},{7,5},{8,10},{9,11},{10,... | collective-permute-start | bytes 393224 | tf_op jit(solution)/shard_map/ppermute | solution.py:177
  66.6 2.2 %collective-permute-start.5 = (f32[64,256]{1,0:T(8,128)S(1)}, f32[64,256]{1,0:T(8,128)S(1)}, u32[]{:S(2)}, u32[]{:S(2)}) collective-permute-start(f32[64,256]{1,0:T(8,128)S(1)} %slice.22), channel_id=1, source_target_pairs={{0,4},{4,8},{8,12},{1,5},{5,9},{9,13},{2,6},{6,10},{10,14},{3,7},{... | collective-permute-start | bytes 196616 | tf_op jit(solution)/shard_map/ppermute | solution.py:262
  73.5 3.3 %collective-permute-start.6 = (bf16[32,8192]{1,0:T(8,128)(2,1)S(1)}, bf16[32,8192]{1,0:T(8,128)(2,1)S(1)}, u32[]{:S(2)}, u32[]{:S(2)}) collective-permute-start(bf16[32,8192]{1,0:T(8,128)(2,1)S(1)} %get-tuple-element.34), channel_id=1, source_target_pairs={{0,4},{4,0},{8,12},{12,8},{1,5},{5,1},{9,13},{13,9},{2,6},{6,2},{1... | collective-permute-start | bytes 1572872 | tf_op jit(solution)/shard_map/ppermute | solution.py:177
  81.0 2.8 %collective-permute-start.8 = (bf16[32,8192]{1,0:T(8,128)(2,1)S(1)}, bf16[32,8192]{1,0:T(8,128)(2,1)S(1)}, u32[]{:S(2)}, u32[]{:S(2)}) collective-permute-start(bf16[32,8192]{1,0:T(8,128)(2,1)S(1)} %get-tuple-element.39), channel_id=1, source_target_pairs={{0,4},{4,0},{8,12},{12,8},{1,5},{5,1},{9,13},{13,9},{2,6},{6,2},{1... | collective-permute-start | bytes 1572872 | tf_op jit(solution)/shard_map/ppermute | solution.py:177
  81.4 9.5 %collective-permute-start.7 = (bf16[16,8192]{1,0:T(8,128)(2,1)S(1)}, bf16[16,8192]{1,0:T(8,128)(2,1)S(1)}, u32[]{:S(2)}, u32[]{:S(2)}) collective-permute-start(bf16[16,8192]{1,0:T(8,128)(2,1)S(1)} %slice.32), channel_id=1, source_target_pairs={{0,8},{4,12},{8,0},{12,4},{1,9},{5,13},{9,1},{13,5},{2,10},{6,14},... | collective-permute-start | bytes 786440 | tf_op jit(solution)/shard_map/ppermute | solution.py:177
  83.9 12.3 %collective-permute-start.9 = (bf16[16,8192]{1,0:T(8,128)(2,1)S(1)}, bf16[16,8192]{1,0:T(8,128)(2,1)S(1)}, u32[]{:S(2)}, u32[]{:S(2)}) collective-permute-start(bf16[16,8192]{1,0:T(8,128)(2,1)S(1)} %slice.31), channel_id=1, source_target_pairs={{0,8},{4,12},{8,0},{12,4},{1,9},{5,13},{9,1},{13,5},{2,10},{6,14},... | collective-permute-start | bytes 786440 | tf_op jit(solution)/shard_map/ppermute | solution.py:177

commit v3 on v2

--- a/solution.py
+++ b/solution.py
@@ -12,13 +12,13 @@
 ORDERS = 256
 ROWS = 256
 COLS = 1024
+LANES = 128
 KERNEL_VMEM = 10 << 20
 SMALL_VMEM = 6 << 20
 INV_TWO_PI = 0.15915494309189535
-TWO_PI_HI = 6.28125
-TWO_PI_LO = 0.0019353071795864769
-COS = (1.0, -1 / 2, 1 / 24, -1 / 720, 1 / 40320, -1 / 3628800, 1 / 479001600, -1 / 87178291200, 1 / 20922789888000)
-SIN = (1.0, -1 / 6, 1 / 120, -1 / 5040, 1 / 362880, -1 / 39916800, 1 / 6227020800, -1 / 1307674368000, 1 / 355687428096000)
+TURN = 12582912.0
+COS = (0.9999992251396179, -19.738981246948242, 64.92865753173828, -85.27162170410156, 58.79049301147461, -21.07110595703125)
+SIN = (6.283185005187988, -41.341590881347656, 81.59994506835938, -76.61447143554688, 41.3428840637207, -12.471243858337402)
 BF16 = jnp.bfloat16
 F32 = jnp.float32
 
@@ -38,50 +38,52 @@
     return lax.dot_general(a, b, (((1,), (1,)), ((), ())), preferred_element_type=F32)
 
 
-def column(row_ref):
-    row = row_ref[...].astype(F32)
-    return jnp.transpose(jnp.broadcast_to(row, (8, row.shape[1])))[:, :1]
-
-
-def fill_tables(bin_ref, frac_ref, lon_ref, weights_ref, trig_ref):
+def spread(row):
+    return jnp.transpose(jnp.broadcast_to(row, (LANES, row.shape[1])))
+
+
+def fraction_of(turns):
+    return turns - ((turns + TURN) - TURN)
+
+
+def trig_kernel(bin_ref, frac_ref, lon_ref, weights_ref, trig_ref):
     nodes = weights_ref.shape[1]
-    bins, fraction, angles = column(bin_ref), column(frac_ref), column(lon_ref)
-    node = lax.broadcasted_iota(jnp.int32, (1, nodes), 1).astype(F32)
-    order = lax.broadcasted_iota(jnp.int32, (1, ORDERS), 1).astype(F32)
-    for first in range(0, weights_ref.shape[0], ROWS):
-        rows = slice(first, first + ROWS)
-        b, f = bins[rows], fraction[rows]
-        lower = jnp.where(node == b, 1.0 - f, 0.0)
-        upper = jnp.where(node == b + 1.0, f, 0.0)
-        weights_ref[rows, :] = (lower + upper).astype(BF16)
-        angle = angles[rows] * order
-        turns = jnp.round(angle * INV_TWO_PI)
-        rest = (angle - turns * TWO_PI_HI) - turns * TWO_PI_LO
-        square = rest * rest
-        trig_ref[rows, :ORDERS] = horner(COS, square).astype(BF16)
-        trig_ref[rows, ORDERS:] = (rest * horner(SIN, square)).astype(BF16)
-
-
-def design_tile(weights_ref, trig_ref, legendre_ref, rows, chosen):
-    interp = dot(weights_ref[rows, :], legendre_ref[...])
-    phases = dot(trig_ref[rows, :], chosen)
-    return (interp * phases).astype(BF16)
-
-
-def one_hot(code_ref):
-    code = code_ref[...]
+    lane = lax.broadcasted_iota(jnp.int32, (1, LANES), 1).astype(F32)
+    for first in range(0, weights_ref.shape[0], LANES):
+        rows = slice(first, first + LANES)
+        bins, fraction = spread(bin_ref[:, rows].astype(F32)), spread(frac_ref[:, rows])
+        lower, upper = 1.0 - fraction, fraction
+        for at in range(0, nodes, LANES):
+            distance = bins - (lane + at)
+            value = jnp.where(distance == 0.0, lower, jnp.where(distance == -1.0, upper, 0.0))
+            weights_ref[rows, at : at + LANES] = value.astype(BF16)
+        turns_row = lon_ref[:, rows] * INV_TWO_PI
+        turns = spread(turns_row)
+        rest, far = fraction_of(turns * lane), fraction_of(turns_row * LANES)
+        square, far_square = rest * rest, far * far
+        cos, sin = horner(COS, square), rest * horner(SIN, square)
+        far_cos, far_sin = spread(horner(COS, far_square)), spread(far * horner(SIN, far_square))
+        for part in range(ORDERS // LANES):
+            if part:
+                cos, sin = cos * far_cos - sin * far_sin, sin * far_cos + cos * far_sin
+            at = part * LANES
+            trig_ref[rows, at : at + LANES] = cos.astype(BF16)
+            trig_ref[rows, ORDERS + at : ORDERS + at + LANES] = sin.astype(BF16)
+
+
+def one_hot(code):
     place = lax.shift_right_logical(code, 1) + (code & 1) * ORDERS
     index = lax.broadcasted_iota(jnp.int32, (2 * ORDERS, 1), 0)
     return jnp.where(index == place, 1.0, 0.0).astype(BF16)
 
 
-def first_kernel(bin_ref, frac_ref, lon_ref, code_ref, legendre_ref, design_ref, weights_ref, trig_ref):
-    @pl.when(pl.program_id(0) == 0)
-    def _():
-        fill_tables(bin_ref, frac_ref, lon_ref, weights_ref, trig_ref)
-
+def design_tile(weights_ref, trig_ref, legendre_ref, rows, chosen):
+    return (dot(weights_ref[rows, :], legendre_ref[...]) * dot(trig_ref[rows, :], chosen)).astype(BF16)
+
+
+def first_kernel(weights_ref, trig_ref, code_ref, legendre_ref, design_ref):
     step = pl.program_id(0)
-    chosen = one_hot(code_ref)
+    chosen = one_hot(code_ref[...])
     for first in range(0, design_ref.shape[1], ROWS):
         rows = slice(first, first + ROWS)
         design_ref[step, rows, :] = design_tile(weights_ref, trig_ref, legendre_ref, rows, chosen)
@@ -98,7 +100,7 @@
 
     probes = jnp.concatenate([ref[...] for ref in probe_refs], axis=0)
     old_probes = jnp.concatenate([ref[...] for ref in old_probe_refs], axis=0)
-    chosen = one_hot(code_ref)
+    chosen = one_hot(code_ref[...])
     for first in range(0, design_ref.shape[1], ROWS):
         rows = slice(first, first + ROWS)
         tile = design_tile(weights_ref, trig_ref, legendre_ref, rows, chosen)
@@ -164,6 +166,10 @@
     return pl.BlockSpec((rows, cols), lambda c: (0, c + shift))
 
 
+def in_hbm(array):
+    return pltpu.with_memory_space_constraint(array, pltpu.HBM)
+
+
 def resident(array):
     return pltpu.with_memory_space_constraint(array, pltpu.VMEM)
 
@@ -187,7 +193,7 @@
     epoch_bits = bits_of("epoch")
     row = lambda array: array.reshape(1, -1)
     codes = row(order_code)
-    legendre = pltpu.with_memory_space_constraint(legendre, pltpu.HBM)
+    legendre, codes = in_hbm(legendre), in_hbm(codes)
     half = coeffs // 2
     cols = min(COLS, half)
     steps = half // cols
@@ -205,24 +211,36 @@
         name="tables",
     )(seg_filter, taps)
 
+    weights, trig = pl.pallas_call(
+        trig_kernel,
+        grid=(1,),
+        in_specs=[whole((1, epochs))] * 3,
+        out_specs=[vmem] * 2,
+        out_shape=[
+            pltpu.VMEM((epochs, nodes), BF16),
+            pltpu.VMEM((epochs, 2 * ORDERS), BF16),
+        ],
+        cost_estimate=cost(40 * epochs * ORDERS, 12 * epochs),
+        compiler_params=pltpu.CompilerParams(vmem_limit_bytes=SMALL_VMEM),
+        name="trig",
+    )(in_hbm(row(lat_bin)), in_hbm(row(lat_frac)), in_hbm(row(longitude)))
+    probes, weights = lax.optimization_barrier((probes, weights))
+    angular = [resident(weights), resident(trig)]
+
     blocks = [probes]
     for bit in reversed(epoch_bits[1:]):
         blocks += [swapped(block, "epoch", bit) for block in blocks]
 
-    design_1, weights, trig = pl.pallas_call(
+    design_1 = pl.pallas_call(
         first_kernel,
         grid=(steps,),
-        in_specs=[whole((1, epochs))] * 3 + [across(1, cols), across(nodes, cols)],
-        out_specs=[vmem, whole((epochs, nodes)), whole((epochs, 2 * ORDERS))],
-        out_shape=[
-            pltpu.VMEM((steps, epochs, cols), BF16),
-            struct((epochs, nodes), BF16),
-            struct((epochs, 2 * ORDERS), BF16),
-        ],
-        cost_estimate=cost(2 * epochs * half * (nodes + 2 * ORDERS), 2 * half * (epochs + nodes)),
+        in_specs=[vmem] * 2 + [across(1, cols), across(nodes, cols)],
+        out_specs=vmem,
+        out_shape=pltpu.VMEM((steps, epochs, cols), BF16),
+        cost_estimate=cost(2 * epochs * half * (nodes + 2 * ORDERS), 2 * half * nodes),
         compiler_params=pltpu.CompilerParams(vmem_limit_bytes=KERNEL_VMEM),
         name="design_first",
-    )(row(lat_bin), row(lat_frac), row(longitude), codes, legendre)
+    )(*angular, codes, legendre)
     blocks, design_1 = lax.optimization_barrier((blocks, design_1))
     blocks = blocks + [swapped(block, "epoch", epoch_bits[0]) for block in blocks]
     count = own * len(blocks)
@@ -234,8 +252,8 @@
         functools.partial(second_kernel, len(blocks)),
         grid=(steps,),
         in_specs=[
-            whole((epochs, nodes)),
-            whole((epochs, 2 * ORDERS)),
+            vmem,
+            vmem,
             across(1, cols, steps),
             across(nodes, cols, steps),
             vmem,
@@ -252,7 +270,7 @@
         cost_estimate=cost(2 * epochs * half * (nodes + 2 * ORDERS + 2 * count), 2 * half * (2 * epochs + nodes)),
         compiler_params=pltpu.CompilerParams(vmem_limit_bytes=KERNEL_VMEM),
         name="design_second",
-    )(weights, trig, codes, legendre, resident(design_1), *blocks, *blocks)
+    )(*angular, codes, legendre, resident(design_1), *blocks, *blocks)
 
     for bit in bits_of("param"):
         pred = pred + swapped(sent, "param", bit).astype(F32)

time: 97.7 us -> 94.1 us (0.963)
  local copies, waits for them, and re-layouts: 2.98 us -> 0.09 us
    unnamed x14 -> x6, local copies, waits for them, and re-layouts: 2.91 us -> 0.02 us
    pallas_call x1 -> x2, Pallas kernels: 18.4 us -> 17.7 us  [the longest x1 16 us: local(): pl.pallas_call(first_kernel, grid=(steps,), in_specs=[vmem] * 2 + [across...]
  transfers between devices with their start and end apart: 10 -> 10, of which waited for: 7 -> 7; matrix products, arithmetic and copies ran while one was open for 0% -> 0% of each run, Pallas kernels for 20% -> 18%
where the time goes in v3:
time: 94.1 us; the launch traced here: 93.8 us
  Pallas kernels  52.6 us (56%)
  waiting for transfers between devices  23.9 us (25%)
  starting transfers between devices  15.6 us (17%)
  other arithmetic  1.4 us (1%)
    pallas_call x1, Pallas kernels, local(): pl.pallas_call(functools.partial(second_kernel, len(blocks)), grid=(steps...  25.3 us
    ppermute x9, waiting for transfers between devices, swapped(): return lax.ppermute(array, axis, [(i, i ^ bit) for i in range(size)])  23.9 us
    pallas_call x1, Pallas kernels, local(): pl.pallas_call(first_kernel, grid=(steps,), in_specs=[vmem] * 2 + [across...  16 us
    ppermute x9, starting transfers between devices, swapped(): return lax.ppermute(array, axis, [(i, i ^ bit) for i in range(size)])  14.4 us
    pallas_call x2, Pallas kernels, local(): pl.pallas_call(residual_kernel, grid=(steps,), in_specs=[whole((count, ep...  8.01 us
  transfers between devices with their start and end apart: 10, of which 7 were waited for; matrix products, arithmetic and copies ran while one was open for 0% of the time, Pallas kernels for 18%

profile of v3, /device:TPU:0, one launch (start us, length us, event | category | flops | bytes accessed | tf_op | source)
XLA Modules:
  0.0 93.8 jit_solution(8690831577522564204)
XLA Ops:
  0.0 1.7 %trig.1 = (bf16[1024,256]{1,0:T(8,128)(2,1)S(1)}, bf16[1024,512]{1,0:T(8,128)(2,1)S(1)}) custom-call(s32[1,1024]{1,0:T(1,128)} %bitcast.6, f32[1,1024]{1,0:T(1,128)} %bitcast.7, f32[1,1024]{1,0:T(1,128)} %bitcast.8), custom_call_target="tpu_custom_call" | custom-call | flops 10485760 | bytes 12288 | tf_op jit(solution)/shard_map/trig/pallas_call | solution.py:214
  1.7 3.1 %collective-permute-start = (bf16[16,16384]{1,0:T(8,128)(2,1)}, bf16[16,16384]{1,0:T(8,128)(2,1)S(1)}, u32[]{:S(2)}, u32[]{:S(2)}) collective-permute-start(bf16[16,16384]{1,0:T(8,128)(2,1)} %refs_4_), channel_id=1, source_target_pairs={{0,8},{4,12},{8,0},{12,4},{1,9},{5,13},{9,1},{13,5},{2,10},{6,14},... | collective-permute-start | bytes 1572872 | tf_op jit(solution)/shard_map/ppermute | solution.py:183
  4.8 0.0 copy-start
  4.8 16.0 %design_first.1.old_ref.design_ref = bf16[8,1024,1024]{2,1,0:T(8,128)(2,1)S(1)} custom-call(bf16[1024,256]{1,0:T(8,128)(2,1)S(1)} %get-tuple-element.25.weights_ref, bf16[1024,512]{1,0:T(8,128)(2,1)S(1)} %get-tuple-element.26.trig_ref, s32[1,16384]{1,0:T(1,128)} %bitcast.4, bf16[256,16384]{1,0:T(8,128)(2,1)} %legendre_ref.3), custom_call_target="tpu_custom_call" | custom-call | flops 12884901888 | bytes 4194304 | tf_op jit(solution)/shard_map/design_first/pallas_call | solution.py:234
  20.8 0.0 copy-start.2
  20.8 0.0 copy-start.1
  20.8 0.0 collective-permute-done.refs_1_.refs_5_
  20.8 0.0 copy-done
  20.8 0.1 collective-permute-start.1
  20.9 0.5 collective-permute-start.2
  21.4 1.4 %collective-permute-done.1.refs_2_.refs_6_ = bf16[16,16384]{1,0:T(8,128)(2,1)S(1)} collective-permute-done((bf16[16,16384]{1,0:T(8,128)(2,1)S(1)}, bf16[16,16384]{1,0:T(8,128)(2,1)S(1)}, u32[]{:S(2)}, u32[]{:S(2)}) %collective-permute-start.1) | collective-permute-done | bytes 524320 | tf_op jit(solution)/shard_map/ppermute | solution.py:183
  22.8 0.7 collective-permute-done.2.refs_3_.refs_7_
  23.6 25.3 %design_second.1 = (bf16[8,1024,1024]{2,1,0:T(8,128)(2,1)S(1)}, f32[64,1024]{1,0:T(8,128)S(1)}, bf16[64,1024]{1,0:T(8,128)(2,1)S(1)}) custom-call(bf16[1024,256]{1,0:T(8,128)(2,1)S(1)} %get-tuple-element.25.weights_ref, bf16[1024,512]{1,0:T(8,128)(2,1)S(1)} %get-tuple-element.26.trig_ref, s32[1,16384]{1,0:T(1,128)} %bitcast.5, ...), custom_call_target="tpu_custom_call" | custom-call | flops 15032385536 | bytes 37748736 | tf_op jit(solution)/shard_map/design_second/pallas_call | solution.py:251
  48.9 1.6 %collective-permute-start.3 = (bf16[64,1024]{1,0:T(8,128)(2,1)S(1)}, bf16[64,1024]{1,0:T(8,128)(2,1)S(1)}, u32[]{:S(2)}, u32[]{:S(2)}) collective-permute-start(bf16[64,1024]{1,0:T(8,128)(2,1)S(1)} %get-tuple-element.32), channel_id=1, source_target_pairs={{0,1},{1,0},{2,3},{3,2},{4,5},{5,4},{6,7},{7,6},{8,9},{9,8},{10,11... | collective-permute-start | bytes 393224 | tf_op jit(solution)/shard_map/ppermute | solution.py:183
  50.5 4.0 %collective-permute-done.3 = bf16[64,1024]{1,0:T(8,128)(2,1)S(1)} collective-permute-done((bf16[64,1024]{1,0:T(8,128)(2,1)S(1)}, bf16[64,1024]{1,0:T(8,128)(2,1)S(1)}, u32[]{:S(2)}, u32[]{:S(2)}) %collective-permute-start.3) | collective-permute-done | bytes 131104 | tf_op jit(solution)/shard_map/ppermute | solution.py:183
  54.5 2.7 %collective-permute-start.4 = (bf16[64,1024]{1,0:T(8,128)(2,1)S(1)}, bf16[64,1024]{1,0:T(8,128)(2,1)S(1)}, u32[]{:S(2)}, u32[]{:S(2)}) collective-permute-start(bf16[64,1024]{1,0:T(8,128)(2,1)S(1)} %fusion), channel_id=1, source_target_pairs={{0,2},{1,3},{2,0},{3,1},{4,6},{5,7},{6,4},{7,5},{8,10},{9,11},{10,... | collective-permute-start | bytes 393224 | tf_op jit(solution)/shard_map/ppermute | solution.py:183
  57.2 5.8 %collective-permute-done.4 = bf16[64,1024]{1,0:T(8,128)(2,1)S(1)} collective-permute-done((bf16[64,1024]{1,0:T(8,128)(2,1)S(1)}, bf16[64,1024]{1,0:T(8,128)(2,1)S(1)}, u32[]{:S(2)}, u32[]{:S(2)}) %collective-permute-start.4) | collective-permute-done | bytes 131104 | tf_op jit(solution)/shard_map/ppermute | solution.py:183
  63.1 1.3 %collective-permute-start.5 = (f32[64,256]{1,0:T(8,128)S(1)}, f32[64,256]{1,0:T(8,128)S(1)}, u32[]{:S(2)}, u32[]{:S(2)}) collective-permute-start(f32[64,256]{1,0:T(8,128)S(1)} %slice.22), channel_id=1, source_target_pairs={{0,4},{4,8},{8,12},{1,5},{5,9},{9,13},{2,6},{6,10},{10,14},{3,7},{... | collective-permute-start | bytes 196616 | tf_op jit(solution)/shard_map/ppermute | solution.py:280
  64.4 0.0 copy-done.2
  64.4 0.0 copy-done.1
  64.4 0.9 tables.1
  65.3 0.0 collective-permute-done.5.before_ref
  65.3 0.7 filter.1.filtered_ref
  66.0 4.0 %residual.2 = (f32[32,8192]{1,0:T(8,128)S(1)}, bf16[32,8192]{1,0:T(8,128)(2,1)S(1)}) custom-call(bf16[64,1024]{1,0:T(8,128)(2,1)S(1)} %filter.1.filtered_ref, bf16[8,1024,1024]{2,1,0:T(8,128)(2,1)S(1)} %design_first.1.old_ref.design_ref), custom_call_target="tpu_custom_call" | custom-call | flops 1073741824 | bytes 3145728 | tf_op jit(solution)/shard_map/residual/pallas_call | solution.py:293
  70.0 1.8 %collective-permute-start.6 = (bf16[32,8192]{1,0:T(8,128)(2,1)S(1)}, bf16[32,8192]{1,0:T(8,128)(2,1)S(1)}, u32[]{:S(2)}, u32[]{:S(2)}) collective-permute-start(bf16[32,8192]{1,0:T(8,128)(2,1)S(1)} %get-tuple-element.36), channel_id=1, source_target_pairs={{0,4},{4,0},{8,12},{12,8},{1,5},{5,1},{9,13},{13,9},{2,6},{6,2},{1... | collective-permute-start | bytes 1572872 | tf_op jit(solution)/shard_map/ppermute | solution.py:183
  71.8 1.5 %collective-permute-done.6 = bf16[32,8192]{1,0:T(8,128)(2,1)S(1)} collective-permute-done((bf16[32,8192]{1,0:T(8,128)(2,1)S(1)}, bf16[32,8192]{1,0:T(8,128)(2,1)S(1)}, u32[]{:S(2)}, u32[]{:S(2)}) %collective-permute-start.6) | collective-permute-done | bytes 524320 | tf_op jit(solution)/shard_map/ppermute | solution.py:183
  73.3 0.1 convert_add_fusion.1
  73.4 4.0 %residual.3 = (f32[32,8192]{1,0:T(8,128)S(1)}, bf16[32,8192]{1,0:T(8,128)(2,1)S(1)}) custom-call(bf16[64,1024]{1,0:T(8,128)(2,1)S(1)} %filter.1.filtered_ref, bf16[8,1024,1024]{2,1,0:T(8,128)(2,1)S(1)} %get-tuple-element.39.design_ref), custom_call_target="tpu_custom_call" | custom-call | flops 1073741824 | bytes 3145728 | tf_op jit(solution)/shard_map/residual/pallas_call | solution.py:293
  77.4 0.4 collective-permute-start.8
  77.9 2.4 %collective-permute-start.7 = (bf16[16,8192]{1,0:T(8,128)(2,1)S(1)}, bf16[16,8192]{1,0:T(8,128)(2,1)S(1)}, u32[]{:S(2)}, u32[]{:S(2)}) collective-permute-start(bf16[16,8192]{1,0:T(8,128)(2,1)S(1)} %slice.32), channel_id=1, source_target_pairs={{0,8},{4,12},{8,0},{12,4},{1,9},{5,13},{9,1},{13,5},{2,10},{6,14},... | collective-permute-start | bytes 786440 | tf_op jit(solution)/shard_map/ppermute | solution.py:183
  80.3 0.0 collective-permute-done.8
  80.3 0.1 convert_add_fusion
  80.4 1.8 %collective-permute-start.9 = (bf16[16,8192]{1,0:T(8,128)(2,1)S(1)}, bf16[16,8192]{1,0:T(8,128)(2,1)S(1)}, u32[]{:S(2)}, u32[]{:S(2)}) collective-permute-start(bf16[16,8192]{1,0:T(8,128)(2,1)S(1)} %slice.31), channel_id=1, source_target_pairs={{0,8},{4,12},{8,0},{12,4},{1,9},{5,13},{9,1},{13,5},{2,10},{6,14},... | collective-permute-start | bytes 786440 | tf_op jit(solution)/shard_map/ppermute | solution.py:183
  82.2 5.2 %collective-permute-done.7 = bf16[16,8192]{1,0:T(8,128)(2,1)S(1)} collective-permute-done((bf16[16,8192]{1,0:T(8,128)(2,1)S(1)}, bf16[16,8192]{1,0:T(8,128)(2,1)S(1)}, u32[]{:S(2)}, u32[]{:S(2)}) %collective-permute-start.7) | collective-permute-done | bytes 262176 | tf_op jit(solution)/shard_map/ppermute | solution.py:183
  87.5 5.3 %collective-permute-done.9 = bf16[16,8192]{1,0:T(8,128)(2,1)S(1)} collective-permute-done((bf16[16,8192]{1,0:T(8,128)(2,1)S(1)}, bf16[16,8192]{1,0:T(8,128)(2,1)S(1)}, u32[]{:S(2)}, u32[]{:S(2)}) %collective-permute-start.9) | collective-permute-done | bytes 262176 | tf_op jit(solution)/shard_map/ppermute | solution.py:183
  92.7 0.1 slice_add_fusion
  92.8 1.0 %pad_maximum_fusion = f32[16,16384]{1,0:T(8,128)} fusion(f32[16,8192]{1,0:T(8,128)S(1)} %slice_add_fusion, f32[16,8192]{1,0:T(8,128)S(1)} %slice_add_fusion.1), kind=kLoop, calls=%fused_computation | loop fusion | flops 262144 | bytes 2097152 | tf_op jit(solution)/shard_map/concatenate | solution.py:310
  (7 shorter events, 0.2 us)
Async XLA Ops:
  1.7 19.1 %collective-permute-start = (bf16[16,16384]{1,0:T(8,128)(2,1)}, bf16[16,16384]{1,0:T(8,128)(2,1)S(1)}, u32[]{:S(2)}, u32[]{:S(2)}) collective-permute-start(bf16[16,16384]{1,0:T(8,128)(2,1)} %refs_4_), channel_id=1, source_target_pairs={{0,8},{4,12},{8,0},{12,4},{1,9},{5,13},{9,1},{13,5},{2,10},{6,14},... | collective-permute-start | bytes 1572872 | tf_op jit(solution)/shard_map/ppermute | solution.py:183
  4.8 16.1 %copy-start = (bf16[16,16384]{1,0:T(8,128)(2,1)S(1)}, bf16[16,16384]{1,0:T(8,128)(2,1)}, u32[]{:S(2)}) copy-start(bf16[16,16384]{1,0:T(8,128)(2,1)} %refs_4_) | copy-start | bytes 1572868
  20.8 43.6 %copy-start.2 = (f32[8,255]{1,0:T(8,128)S(1)}, f32[8,255]{1,0:T(8,128)}, u32[]{:S(2)}) copy-start(f32[8,255]{1,0:T(8,128)} %param.14) | copy-start | bytes 24484
  20.8 43.6 %copy-start.1 = (s32[4]{0:T(128)S(1)}, s32[4]{0:T(128)}, u32[]{:S(2)}) copy-start(s32[4]{0:T(128)} %seg_ref.1) | copy-start | bytes 52
  20.8 2.0 %collective-permute-start.1 = (bf16[16,16384]{1,0:T(8,128)(2,1)S(1)}, bf16[16,16384]{1,0:T(8,128)(2,1)S(1)}, u32[]{:S(2)}, u32[]{:S(2)}) collective-permute-start(bf16[16,16384]{1,0:T(8,128)(2,1)S(1)} %copy-done), channel_id=1, source_target_pairs={{0,4},{4,0},{8,12},{12,8},{1,5},{5,1},{9,13},{13,9},{2,6},{6,2},{1... | collective-permute-start | bytes 1572872 | tf_op jit(solution)/shard_map/ppermute | solution.py:183
  20.9 2.6 %collective-permute-start.2 = (bf16[16,16384]{1,0:T(8,128)(2,1)S(1)}, bf16[16,16384]{1,0:T(8,128)(2,1)S(1)}, u32[]{:S(2)}, u32[]{:S(2)}) collective-permute-start(bf16[16,16384]{1,0:T(8,128)(2,1)S(1)} %collective-permute-done.refs_1_.refs_5_), channel_id=1, source_target_pairs={{0,4},{4,0},{8,12},{12,8},{1,5},{5,1},{9,13},{13,9},{2,6},{6,2},{1... | collective-permute-start | bytes 1572872 | tf_op jit(solution)/shard_map/ppermute | solution.py:183
  48.9 5.6 %collective-permute-start.3 = (bf16[64,1024]{1,0:T(8,128)(2,1)S(1)}, bf16[64,1024]{1,0:T(8,128)(2,1)S(1)}, u32[]{:S(2)}, u32[]{:S(2)}) collective-permute-start(bf16[64,1024]{1,0:T(8,128)(2,1)S(1)} %get-tuple-element.32), channel_id=1, source_target_pairs={{0,1},{1,0},{2,3},{3,2},{4,5},{5,4},{6,7},{7,6},{8,9},{9,8},{10,11... | collective-permute-start | bytes 393224 | tf_op jit(solution)/shard_map/ppermute | solution.py:183
  54.5 8.5 %collective-permute-start.4 = (bf16[64,1024]{1,0:T(8,128)(2,1)S(1)}, bf16[64,1024]{1,0:T(8,128)(2,1)S(1)}, u32[]{:S(2)}, u32[]{:S(2)}) collective-permute-start(bf16[64,1024]{1,0:T(8,128)(2,1)S(1)} %fusion), channel_id=1, source_target_pairs={{0,2},{1,3},{2,0},{3,1},{4,6},{5,7},{6,4},{7,5},{8,10},{9,11},{10,... | collective-permute-start | bytes 393224 | tf_op jit(solution)/shard_map/ppermute | solution.py:183
  63.1 2.2 %collective-permute-start.5 = (f32[64,256]{1,0:T(8,128)S(1)}, f32[64,256]{1,0:T(8,128)S(1)}, u32[]{:S(2)}, u32[]{:S(2)}) collective-permute-start(f32[64,256]{1,0:T(8,128)S(1)} %slice.22), channel_id=1, source_target_pairs={{0,4},{4,8},{8,12},{1,5},{5,9},{9,13},{2,6},{6,10},{10,14},{3,7},{... | collective-permute-start | bytes 196616 | tf_op jit(solution)/shard_map/ppermute | solution.py:280
  70.0 3.3 %collective-permute-start.6 = (bf16[32,8192]{1,0:T(8,128)(2,1)S(1)}, bf16[32,8192]{1,0:T(8,128)(2,1)S(1)}, u32[]{:S(2)}, u32[]{:S(2)}) collective-permute-start(bf16[32,8192]{1,0:T(8,128)(2,1)S(1)} %get-tuple-element.36), channel_id=1, source_target_pairs={{0,4},{4,0},{8,12},{12,8},{1,5},{5,1},{9,13},{13,9},{2,6},{6,2},{1... | collective-permute-start | bytes 1572872 | tf_op jit(solution)/shard_map/ppermute | solution.py:183
  77.4 2.8 %collective-permute-start.8 = (bf16[32,8192]{1,0:T(8,128)(2,1)S(1)}, bf16[32,8192]{1,0:T(8,128)(2,1)S(1)}, u32[]{:S(2)}, u32[]{:S(2)}) collective-permute-start(bf16[32,8192]{1,0:T(8,128)(2,1)S(1)} %get-tuple-element.41), channel_id=1, source_target_pairs={{0,4},{4,0},{8,12},{12,8},{1,5},{5,1},{9,13},{13,9},{2,6},{6,2},{1... | collective-permute-start | bytes 1572872 | tf_op jit(solution)/shard_map/ppermute | solution.py:183
  77.9 9.5 %collective-permute-start.7 = (bf16[16,8192]{1,0:T(8,128)(2,1)S(1)}, bf16[16,8192]{1,0:T(8,128)(2,1)S(1)}, u32[]{:S(2)}, u32[]{:S(2)}) collective-permute-start(bf16[16,8192]{1,0:T(8,128)(2,1)S(1)} %slice.32), channel_id=1, source_target_pairs={{0,8},{4,12},{8,0},{12,4},{1,9},{5,13},{9,1},{13,5},{2,10},{6,14},... | collective-permute-start | bytes 786440 | tf_op jit(solution)/shard_map/ppermute | solution.py:183
  80.4 12.3 %collective-permute-start.9 = (bf16[16,8192]{1,0:T(8,128)(2,1)S(1)}, bf16[16,8192]{1,0:T(8,128)(2,1)S(1)}, u32[]{:S(2)}, u32[]{:S(2)}) collective-permute-start(bf16[16,8192]{1,0:T(8,128)(2,1)S(1)} %slice.31), channel_id=1, source_target_pairs={{0,8},{4,12},{8,0},{12,4},{1,9},{5,13},{9,1},{13,5},{2,10},{6,14},... | collective-permute-start | bytes 786440 | tf_op jit(solution)/shard_map/ppermute | solution.py:183

commit v4 on v3

--- a/solution.py
+++ b/solution.py
@@ -13,6 +13,8 @@
 ROWS = 256
 COLS = 1024
 LANES = 128
+TILE = 256
+FIRST_COMPUTED, SECOND_COMPUTED = (1,), (1, 3)
 KERNEL_VMEM = 10 << 20
 SMALL_VMEM = 6 << 20
 INV_TWO_PI = 0.15915494309189535
@@ -46,7 +48,7 @@
     return turns - ((turns + TURN) - TURN)
 
 
-def trig_kernel(bin_ref, frac_ref, lon_ref, weights_ref, trig_ref):
+def trig_kernel(bin_ref, frac_ref, lon_ref, weights_ref, trig_ref, turns_ref):
     nodes = weights_ref.shape[1]
     lane = lax.broadcasted_iota(jnp.int32, (1, LANES), 1).astype(F32)
     for first in range(0, weights_ref.shape[0], LANES):
@@ -59,6 +61,7 @@
             weights_ref[rows, at : at + LANES] = value.astype(BF16)
         turns_row = lon_ref[:, rows] * INV_TWO_PI
         turns = spread(turns_row)
+        turns_ref[rows, :] = turns
         rest, far = fraction_of(turns * lane), fraction_of(turns_row * LANES)
         square, far_square = rest * rest, far * far
         cos, sin = horner(COS, square), rest * horner(SIN, square)
@@ -77,21 +80,49 @@
     return jnp.where(index == place, 1.0, 0.0).astype(BF16)
 
 
-def design_tile(weights_ref, trig_ref, legendre_ref, rows, chosen):
-    return (dot(weights_ref[rows, :], legendre_ref[...]) * dot(trig_ref[rows, :], chosen)).astype(BF16)
-
-
-def first_kernel(weights_ref, trig_ref, code_ref, legendre_ref, design_ref):
-    step = pl.program_id(0)
-    chosen = one_hot(code_ref[...])
+def build_design(weights_ref, trig_ref, turns_ref, code_ref, legendre_ref, design_ref, phase_ref, step, computed, after):
+    code = code_ref[...]
+    cols = code.shape[1]
+    order = lax.shift_right_logical(code, 1).astype(F32)
+    offset = (code & 1).astype(F32) * -0.25
+    tiles = [slice(at, at + TILE) for at in range(0, cols, TILE)]
+    chosen = {}
+    for n, tile in enumerate(tiles):
+        if n not in computed:
+            chosen[n] = one_hot(code[:, tile])
+
+    def compute(first):
+        rows = slice(first, first + ROWS)
+        for place, n in enumerate(computed):
+            for at in range(0, TILE, LANES):
+                lanes = slice(tiles[n].start + at, tiles[n].start + at + LANES)
+                rest = fraction_of(turns_ref[rows, :] * order[:, lanes] + offset[:, lanes])
+                phase_ref[rows, place * TILE + at : place * TILE + at + LANES] = horner(COS, rest * rest)
+
+    compute(0)
     for first in range(0, design_ref.shape[1], ROWS):
         rows = slice(first, first + ROWS)
-        design_ref[step, rows, :] = design_tile(weights_ref, trig_ref, legendre_ref, rows, chosen)
-
-
-def second_kernel(blocks, weights_ref, trig_ref, code_ref, legendre_ref, old_ref, *refs):
+        if first + ROWS < design_ref.shape[1]:
+            compute(first + ROWS)
+        for n, tile in enumerate(tiles):
+            interp = dot(weights_ref[rows, :], legendre_ref[:, tile])
+            if n in chosen:
+                phase = dot(trig_ref[rows, :], chosen[n])
+            else:
+                place = computed.index(n) * TILE
+                phase = phase_ref[rows, place : place + TILE]
+            design_ref[step, rows, tile] = (interp * phase).astype(BF16)
+        after(rows)
+
+
+def first_kernel(weights_ref, trig_ref, turns_ref, code_ref, legendre_ref, design_ref, phase_ref):
+    step = pl.program_id(0)
+    build_design(weights_ref, trig_ref, turns_ref, code_ref, legendre_ref, design_ref, phase_ref, step, FIRST_COMPUTED, lambda rows: None)
+
+
+def second_kernel(blocks, weights_ref, trig_ref, turns_ref, code_ref, legendre_ref, old_ref, *refs):
     probe_refs, old_probe_refs = refs[:blocks], refs[blocks : 2 * blocks]
-    design_ref, pred_ref, sent_ref, total_ref = refs[2 * blocks :]
+    design_ref, pred_ref, sent_ref, total_ref, phase_ref = refs[2 * blocks :]
     step = pl.program_id(0)
 
     @pl.when(step == 0)
@@ -100,12 +131,11 @@
 
     probes = jnp.concatenate([ref[...] for ref in probe_refs], axis=0)
     old_probes = jnp.concatenate([ref[...] for ref in old_probe_refs], axis=0)
-    chosen = one_hot(code_ref[...])
-    for first in range(0, design_ref.shape[1], ROWS):
-        rows = slice(first, first + ROWS)
-        tile = design_tile(weights_ref, trig_ref, legendre_ref, rows, chosen)
-        design_ref[step, rows, :] = tile
-        total_ref[rows, :] += dot_t(tile, probes) + dot_t(old_ref[step, rows, :], old_probes)
+
+    def predict(rows):
+        total_ref[rows, :] += dot_t(design_ref[step, rows, :], probes) + dot_t(old_ref[step, rows, :], old_probes)
+
+    build_design(weights_ref, trig_ref, turns_ref, code_ref, legendre_ref, design_ref, phase_ref, step, SECOND_COMPUTED, predict)
 
     @pl.when(step == pl.num_programs(0) - 1)
     def _():
@@ -148,10 +178,11 @@
 
 
 def residual_kernel(filtered_ref, design_ref, kept_ref, sent_ref):
-    value = dot(filtered_ref[...], design_ref[pl.program_id(0)])
-    half = kept_ref.shape[0]
-    kept_ref[...] = value[:half]
-    sent_ref[...] = value[half:].astype(BF16)
+    half, cols = kept_ref.shape[0], design_ref.shape[2]
+    for step in range(design_ref.shape[0]):
+        value = dot(filtered_ref[...], design_ref[step])
+        kept_ref[:, step * cols : (step + 1) * cols] = value[:half]
+        sent_ref[:, step * cols : (step + 1) * cols] = value[half:].astype(BF16)
 
 
 def struct(shape, dtype):
@@ -211,21 +242,22 @@
         name="tables",
     )(seg_filter, taps)
 
-    weights, trig = pl.pallas_call(
+    weights, trig, turns = pl.pallas_call(
         trig_kernel,
         grid=(1,),
         in_specs=[whole((1, epochs))] * 3,
-        out_specs=[vmem] * 2,
+        out_specs=[vmem] * 3,
         out_shape=[
             pltpu.VMEM((epochs, nodes), BF16),
             pltpu.VMEM((epochs, 2 * ORDERS), BF16),
+            pltpu.VMEM((epochs, LANES), F32),
         ],
         cost_estimate=cost(40 * epochs * ORDERS, 12 * epochs),
         compiler_params=pltpu.CompilerParams(vmem_limit_bytes=SMALL_VMEM),
         name="trig",
     )(in_hbm(row(lat_bin)), in_hbm(row(lat_frac)), in_hbm(row(longitude)))
     probes, weights = lax.optimization_barrier((probes, weights))
-    angular = [resident(weights), resident(trig)]
+    angular = [resident(weights), resident(trig), resident(turns)]
 
     blocks = [probes]
     for bit in reversed(epoch_bits[1:]):
@@ -234,9 +266,10 @@
     design_1 = pl.pallas_call(
         first_kernel,
         grid=(steps,),
-        in_specs=[vmem] * 2 + [across(1, cols), across(nodes, cols)],
+        in_specs=[vmem] * 3 + [across(1, cols), across(nodes, cols)],
         out_specs=vmem,
         out_shape=pltpu.VMEM((steps, epochs, cols), BF16),
+        scratch_shapes=[pltpu.VMEM((epochs, TILE * len(FIRST_COMPUTED)), F32)],
         cost_estimate=cost(2 * epochs * half * (nodes + 2 * ORDERS), 2 * half * nodes),
         compiler_params=pltpu.CompilerParams(vmem_limit_bytes=KERNEL_VMEM),
         name="design_first",
@@ -252,6 +285,7 @@
         functools.partial(second_kernel, len(blocks)),
         grid=(steps,),
         in_specs=[
+            vmem,
             vmem,
             vmem,
             across(1, cols, steps),
@@ -266,7 +300,7 @@
             struct((count, epochs), F32),
             struct((count, epochs), BF16),
         ],
-        scratch_shapes=[pltpu.VMEM((epochs, count), F32)],
+        scratch_shapes=[pltpu.VMEM((epochs, count), F32), pltpu.VMEM((epochs, TILE * len(SECOND_COMPUTED)), F32)],
         cost_estimate=cost(2 * epochs * half * (nodes + 2 * ORDERS + 2 * count), 2 * half * (2 * epochs + nodes)),
         compiler_params=pltpu.CompilerParams(vmem_limit_bytes=KERNEL_VMEM),
         name="design_second",
@@ -292,10 +326,9 @@
     for design in (design_1, design_2):
         kept, sent = pl.pallas_call(
             residual_kernel,
-            grid=(steps,),
-            in_specs=[whole((count, epochs)), vmem],
-            out_specs=[across(count // 2, cols)] * 2,
-            out_shape=[struct((count // 2, half), F32), struct((count // 2, half), BF16)],
+            in_specs=[vmem] * 2,
+            out_specs=[vmem] * 2,
+            out_shape=[pltpu.VMEM((count // 2, half), F32), pltpu.VMEM((count // 2, half), BF16)],
             cost_estimate=cost(2 * count * epochs * half, 6 * count * half),
             compiler_params=pltpu.CompilerParams(vmem_limit_bytes=SMALL_VMEM),
             name="residual",

time: 94.1 us -> 89.2 us (0.948)
  Pallas kernels: 52.6 us -> 47.7 us
    pallas_call x3, Pallas kernels: 24 us -> 20.9 us  [the longest x1 14.9 us: local(): pl.pallas_call(first_kernel, grid=(steps,), in_specs=[vmem] * 3 + [across...]
    pallas_call x1, Pallas kernels: 25.3 us -> 23.5 us  [local(): pl.pallas_call(functools.partial(second_kernel, len(blocks)), grid=(steps...]
where the time goes in v4:
time: 89.2 us; the launch traced here: 88.9 us
  Pallas kernels  47.7 us (53%)
  waiting for transfers between devices  23.9 us (27%)
  starting transfers between devices  15.6 us (17%)
  other arithmetic  1.4 us (2%)
    ppermute x9, waiting for transfers between devices, swapped(): return lax.ppermute(array, axis, [(i, i ^ bit) for i in range(size)])  23.9 us
    pallas_call x1, Pallas kernels, local(): pl.pallas_call(functools.partial(second_kernel, len(blocks)), grid=(steps...  23.5 us
    pallas_call x1, Pallas kernels, local(): pl.pallas_call(first_kernel, grid=(steps,), in_specs=[vmem] * 3 + [across...  14.9 us
    ppermute x9, starting transfers between devices, swapped(): return lax.ppermute(array, axis, [(i, i ^ bit) for i in range(size)])  14.4 us
    pallas_call x2, Pallas kernels, local(): pl.pallas_call(residual_kernel, in_specs=[vmem] * 2, out_specs=[vmem] * 2...  6.04 us
  transfers between devices with their start and end apart: 10, of which 7 were waited for; matrix products, arithmetic and copies ran while one was open for 0% of the time, Pallas kernels for 18%

profile of v4, /device:TPU:0, one launch (start us, length us, event | category | flops | bytes accessed | tf_op | source)
XLA Modules:
  0.0 88.9 jit_solution(3637512387851663723)
XLA Ops:
  0.0 1.7 %trig.1 = (bf16[1024,256]{1,0:T(8,128)(2,1)S(1)}, bf16[1024,512]{1,0:T(8,128)(2,1)S(1)}, f32[1024,128]{1,0:T(8,128)S(1)}) custom-call(s32[1,1024]{1,0:T(1,128)} %bitcast.6, f32[1,1024]{1,0:T(1,128)} %bitcast.7, f32[1,1024]{1,0:T(1,128)} %bitcast.8), custom_call_target="tpu_custom_call" | custom-call | flops 10485760 | bytes 12288 | tf_op jit(solution)/shard_map/trig/pallas_call | solution.py:245
  1.7 3.1 %collective-permute-start = (bf16[16,16384]{1,0:T(8,128)(2,1)}, bf16[16,16384]{1,0:T(8,128)(2,1)S(1)}, u32[]{:S(2)}, u32[]{:S(2)}) collective-permute-start(bf16[16,16384]{1,0:T(8,128)(2,1)} %refs_4_), channel_id=1, source_target_pairs={{0,8},{4,12},{8,0},{12,4},{1,9},{5,13},{9,1},{13,5},{2,10},{6,14},... | collective-permute-start | bytes 1572872 | tf_op jit(solution)/shard_map/ppermute | solution.py:214
  4.8 0.0 copy-start
  4.8 14.9 %design_first.1.old_ref.design_ref = bf16[8,1024,1024]{2,1,0:T(8,128)(2,1)S(1)} custom-call(bf16[1024,256]{1,0:T(8,128)(2,1)S(1)} %get-tuple-element.26.weights_ref, bf16[1024,512]{1,0:T(8,128)(2,1)S(1)} %get-tuple-element.27.trig_ref, f32[1024,128]{1,0:T(8,128)S(1)} %get-tuple-element.28.turns_ref, s32[1,16384]{1,0:T(1,128)} %bitcast.4, ...), custom_call_target="tpu_custom_call" | custom-call | flops 12884901888 | bytes 4194304 | tf_op jit(solution)/shard_map/design_first/pallas_call | solution.py:266
  19.6 0.0 copy-start.2
  19.7 0.0 copy-start.1
  19.7 0.0 collective-permute-done.refs_1_.refs_5_
  19.7 0.0 copy-done
  19.7 0.1 collective-permute-start.1
  19.8 0.5 collective-permute-start.2
  20.3 1.4 %collective-permute-done.1.refs_2_.refs_6_ = bf16[16,16384]{1,0:T(8,128)(2,1)S(1)} collective-permute-done((bf16[16,16384]{1,0:T(8,128)(2,1)S(1)}, bf16[16,16384]{1,0:T(8,128)(2,1)S(1)}, u32[]{:S(2)}, u32[]{:S(2)}) %collective-permute-start.1) | collective-permute-done | bytes 524320 | tf_op jit(solution)/shard_map/ppermute | solution.py:214
  21.7 0.7 collective-permute-done.2.refs_3_.refs_7_
  22.4 23.5 %design_second.1 = (bf16[8,1024,1024]{2,1,0:T(8,128)(2,1)S(1)}, f32[64,1024]{1,0:T(8,128)S(1)}, bf16[64,1024]{1,0:T(8,128)(2,1)S(1)}) custom-call(bf16[1024,256]{1,0:T(8,128)(2,1)S(1)} %get-tuple-element.26.weights_ref, bf16[1024,512]{1,0:T(8,128)(2,1)S(1)} %get-tuple-element.27.trig_ref, f32[1024,128]{1,0:T(8,128)S(1)} %get-tuple-element.28.turns_ref, ...), custom_call_target="tpu_custom_call" | custom-call | flops 15032385536 | bytes 37748736 | tf_op jit(solution)/shard_map/design_second/pallas_call | solution.py:284
  46.0 1.6 %collective-permute-start.3 = (bf16[64,1024]{1,0:T(8,128)(2,1)S(1)}, bf16[64,1024]{1,0:T(8,128)(2,1)S(1)}, u32[]{:S(2)}, u32[]{:S(2)}) collective-permute-start(bf16[64,1024]{1,0:T(8,128)(2,1)S(1)} %get-tuple-element.34), channel_id=1, source_target_pairs={{0,1},{1,0},{2,3},{3,2},{4,5},{5,4},{6,7},{7,6},{8,9},{9,8},{10,11... | collective-permute-start | bytes 393224 | tf_op jit(solution)/shard_map/ppermute | solution.py:214
  47.6 4.0 %collective-permute-done.3 = bf16[64,1024]{1,0:T(8,128)(2,1)S(1)} collective-permute-done((bf16[64,1024]{1,0:T(8,128)(2,1)S(1)}, bf16[64,1024]{1,0:T(8,128)(2,1)S(1)}, u32[]{:S(2)}, u32[]{:S(2)}) %collective-permute-start.3) | collective-permute-done | bytes 131104 | tf_op jit(solution)/shard_map/ppermute | solution.py:214
  51.6 2.7 %collective-permute-start.4 = (bf16[64,1024]{1,0:T(8,128)(2,1)S(1)}, bf16[64,1024]{1,0:T(8,128)(2,1)S(1)}, u32[]{:S(2)}, u32[]{:S(2)}) collective-permute-start(bf16[64,1024]{1,0:T(8,128)(2,1)S(1)} %fusion), channel_id=1, source_target_pairs={{0,2},{1,3},{2,0},{3,1},{4,6},{5,7},{6,4},{7,5},{8,10},{9,11},{10,... | collective-permute-start | bytes 393224 | tf_op jit(solution)/shard_map/ppermute | solution.py:214
  54.3 5.8 %collective-permute-done.4 = bf16[64,1024]{1,0:T(8,128)(2,1)S(1)} collective-permute-done((bf16[64,1024]{1,0:T(8,128)(2,1)S(1)}, bf16[64,1024]{1,0:T(8,128)(2,1)S(1)}, u32[]{:S(2)}, u32[]{:S(2)}) %collective-permute-start.4) | collective-permute-done | bytes 131104 | tf_op jit(solution)/shard_map/ppermute | solution.py:214
  60.1 1.3 %collective-permute-start.5 = (f32[64,256]{1,0:T(8,128)S(1)}, f32[64,256]{1,0:T(8,128)S(1)}, u32[]{:S(2)}, u32[]{:S(2)}) collective-permute-start(f32[64,256]{1,0:T(8,128)S(1)} %slice.22), channel_id=1, source_target_pairs={{0,4},{4,8},{8,12},{1,5},{5,9},{9,13},{2,6},{6,10},{10,14},{3,7},{... | collective-permute-start | bytes 196616 | tf_op jit(solution)/shard_map/ppermute | solution.py:314
  61.4 0.0 copy-done.2
  61.4 0.0 copy-done.1
  61.5 0.9 %tables.1 = (bf16[4,512,256]{2,1,0:T(8,128)(2,1)S(1)}, bf16[4,512,256]{2,1,0:T(8,128)(2,1)S(1)}) custom-call(s32[4]{0:T(128)S(1)} %copy-done.1, f32[8,512]{1,0:T(8,128)S(1)} %pad.4.bank_ref), custom_call_target="tpu_custom_call" | custom-call | flops 10485760 | bytes 2097152 | tf_op jit(solution)/shard_map/tables/pallas_call | solution.py:235
  62.4 0.0 collective-permute-done.5.before_ref
  62.4 0.7 filter.1.filtered_ref
  63.0 3.0 %residual.2 = (f32[32,8192]{1,0:T(8,128)S(1)}, bf16[32,8192]{1,0:T(8,128)(2,1)S(1)}) custom-call(bf16[64,1024]{1,0:T(8,128)(2,1)S(1)} %filter.1.filtered_ref, bf16[8,1024,1024]{2,1,0:T(8,128)(2,1)S(1)} %design_first.1.old_ref.design_ref), custom_call_target="tpu_custom_call" | custom-call | flops 1073741824 | bytes 3145728 | tf_op jit(solution)/shard_map/residual/pallas_call | solution.py:327
  66.1 1.8 %collective-permute-start.6 = (bf16[32,8192]{1,0:T(8,128)(2,1)S(1)}, bf16[32,8192]{1,0:T(8,128)(2,1)S(1)}, u32[]{:S(2)}, u32[]{:S(2)}) collective-permute-start(bf16[32,8192]{1,0:T(8,128)(2,1)S(1)} %get-tuple-element.38), channel_id=1, source_target_pairs={{0,4},{4,0},{8,12},{12,8},{1,5},{5,1},{9,13},{13,9},{2,6},{6,2},{1... | collective-permute-start | bytes 1572872 | tf_op jit(solution)/shard_map/ppermute | solution.py:214
  67.8 1.5 %collective-permute-done.6 = bf16[32,8192]{1,0:T(8,128)(2,1)S(1)} collective-permute-done((bf16[32,8192]{1,0:T(8,128)(2,1)S(1)}, bf16[32,8192]{1,0:T(8,128)(2,1)S(1)}, u32[]{:S(2)}, u32[]{:S(2)}) %collective-permute-start.6) | collective-permute-done | bytes 524320 | tf_op jit(solution)/shard_map/ppermute | solution.py:214
  69.4 0.1 convert_add_fusion.1
  69.5 3.0 %residual.3 = (f32[32,8192]{1,0:T(8,128)S(1)}, bf16[32,8192]{1,0:T(8,128)(2,1)S(1)}) custom-call(bf16[64,1024]{1,0:T(8,128)(2,1)S(1)} %filter.1.filtered_ref, bf16[8,1024,1024]{2,1,0:T(8,128)(2,1)S(1)} %get-tuple-element.41.design_ref), custom_call_target="tpu_custom_call" | custom-call | flops 1073741824 | bytes 3145728 | tf_op jit(solution)/shard_map/residual/pallas_call | solution.py:327
  72.5 0.4 collective-permute-start.8
  73.0 2.4 %collective-permute-start.7 = (bf16[16,8192]{1,0:T(8,128)(2,1)S(1)}, bf16[16,8192]{1,0:T(8,128)(2,1)S(1)}, u32[]{:S(2)}, u32[]{:S(2)}) collective-permute-start(bf16[16,8192]{1,0:T(8,128)(2,1)S(1)} %slice.32), channel_id=1, source_target_pairs={{0,8},{4,12},{8,0},{12,4},{1,9},{5,13},{9,1},{13,5},{2,10},{6,14},... | collective-permute-start | bytes 786440 | tf_op jit(solution)/shard_map/ppermute | solution.py:214
  75.4 0.0 collective-permute-done.8
  75.4 0.1 convert_add_fusion
  75.5 1.8 %collective-permute-start.9 = (bf16[16,8192]{1,0:T(8,128)(2,1)S(1)}, bf16[16,8192]{1,0:T(8,128)(2,1)S(1)}, u32[]{:S(2)}, u32[]{:S(2)}) collective-permute-start(bf16[16,8192]{1,0:T(8,128)(2,1)S(1)} %slice.31), channel_id=1, source_target_pairs={{0,8},{4,12},{8,0},{12,4},{1,9},{5,13},{9,1},{13,5},{2,10},{6,14},... | collective-permute-start | bytes 786440 | tf_op jit(solution)/shard_map/ppermute | solution.py:214
  77.3 5.2 %collective-permute-done.7 = bf16[16,8192]{1,0:T(8,128)(2,1)S(1)} collective-permute-done((bf16[16,8192]{1,0:T(8,128)(2,1)S(1)}, bf16[16,8192]{1,0:T(8,128)(2,1)S(1)}, u32[]{:S(2)}, u32[]{:S(2)}) %collective-permute-start.7) | collective-permute-done | bytes 262176 | tf_op jit(solution)/shard_map/ppermute | solution.py:214
  82.6 5.3 %collective-permute-done.9 = bf16[16,8192]{1,0:T(8,128)(2,1)S(1)} collective-permute-done((bf16[16,8192]{1,0:T(8,128)(2,1)S(1)}, bf16[16,8192]{1,0:T(8,128)(2,1)S(1)}, u32[]{:S(2)}, u32[]{:S(2)}) %collective-permute-start.9) | collective-permute-done | bytes 262176 | tf_op jit(solution)/shard_map/ppermute | solution.py:214
  87.8 0.1 slice_add_fusion
  87.9 1.0 %pad_maximum_fusion = f32[16,16384]{1,0:T(8,128)} fusion(f32[16,8192]{1,0:T(8,128)S(1)} %slice_add_fusion, f32[16,8192]{1,0:T(8,128)S(1)} %slice_add_fusion.1), kind=kLoop, calls=%fused_computation | loop fusion | flops 262144 | bytes 2097152 | tf_op jit(solution)/shard_map/concatenate | solution.py:343
  (7 shorter events, 0.2 us)
Async XLA Ops:
  1.7 18.0 %collective-permute-start = (bf16[16,16384]{1,0:T(8,128)(2,1)}, bf16[16,16384]{1,0:T(8,128)(2,1)S(1)}, u32[]{:S(2)}, u32[]{:S(2)}) collective-permute-start(bf16[16,16384]{1,0:T(8,128)(2,1)} %refs_4_), channel_id=1, source_target_pairs={{0,8},{4,12},{8,0},{12,4},{1,9},{5,13},{9,1},{13,5},{2,10},{6,14},... | collective-permute-start | bytes 1572872 | tf_op jit(solution)/shard_map/ppermute | solution.py:214
  4.8 14.9 %copy-start = (bf16[16,16384]{1,0:T(8,128)(2,1)S(1)}, bf16[16,16384]{1,0:T(8,128)(2,1)}, u32[]{:S(2)}) copy-start(bf16[16,16384]{1,0:T(8,128)(2,1)} %refs_4_) | copy-start | bytes 1572868
  19.6 41.8 %copy-start.2 = (f32[8,255]{1,0:T(8,128)S(1)}, f32[8,255]{1,0:T(8,128)}, u32[]{:S(2)}) copy-start(f32[8,255]{1,0:T(8,128)} %param.14) | copy-start | bytes 24484
  19.7 41.8 %copy-start.1 = (s32[4]{0:T(128)S(1)}, s32[4]{0:T(128)}, u32[]{:S(2)}) copy-start(s32[4]{0:T(128)} %seg_ref.1) | copy-start | bytes 52
  19.7 2.0 %collective-permute-start.1 = (bf16[16,16384]{1,0:T(8,128)(2,1)S(1)}, bf16[16,16384]{1,0:T(8,128)(2,1)S(1)}, u32[]{:S(2)}, u32[]{:S(2)}) collective-permute-start(bf16[16,16384]{1,0:T(8,128)(2,1)S(1)} %copy-done), channel_id=1, source_target_pairs={{0,4},{4,0},{8,12},{12,8},{1,5},{5,1},{9,13},{13,9},{2,6},{6,2},{1... | collective-permute-start | bytes 1572872 | tf_op jit(solution)/shard_map/ppermute | solution.py:214
  19.8 2.6 %collective-permute-start.2 = (bf16[16,16384]{1,0:T(8,128)(2,1)S(1)}, bf16[16,16384]{1,0:T(8,128)(2,1)S(1)}, u32[]{:S(2)}, u32[]{:S(2)}) collective-permute-start(bf16[16,16384]{1,0:T(8,128)(2,1)S(1)} %collective-permute-done.refs_1_.refs_5_), channel_id=1, source_target_pairs={{0,4},{4,0},{8,12},{12,8},{1,5},{5,1},{9,13},{13,9},{2,6},{6,2},{1... | collective-permute-start | bytes 1572872 | tf_op jit(solution)/shard_map/ppermute | solution.py:214
  46.0 5.6 %collective-permute-start.3 = (bf16[64,1024]{1,0:T(8,128)(2,1)S(1)}, bf16[64,1024]{1,0:T(8,128)(2,1)S(1)}, u32[]{:S(2)}, u32[]{:S(2)}) collective-permute-start(bf16[64,1024]{1,0:T(8,128)(2,1)S(1)} %get-tuple-element.34), channel_id=1, source_target_pairs={{0,1},{1,0},{2,3},{3,2},{4,5},{5,4},{6,7},{7,6},{8,9},{9,8},{10,11... | collective-permute-start | bytes 393224 | tf_op jit(solution)/shard_map/ppermute | solution.py:214
  51.6 8.5 %collective-permute-start.4 = (bf16[64,1024]{1,0:T(8,128)(2,1)S(1)}, bf16[64,1024]{1,0:T(8,128)(2,1)S(1)}, u32[]{:S(2)}, u32[]{:S(2)}) collective-permute-start(bf16[64,1024]{1,0:T(8,128)(2,1)S(1)} %fusion), channel_id=1, source_target_pairs={{0,2},{1,3},{2,0},{3,1},{4,6},{5,7},{6,4},{7,5},{8,10},{9,11},{10,... | collective-permute-start | bytes 393224 | tf_op jit(solution)/shard_map/ppermute | solution.py:214
  60.1 2.2 %collective-permute-start.5 = (f32[64,256]{1,0:T(8,128)S(1)}, f32[64,256]{1,0:T(8,128)S(1)}, u32[]{:S(2)}, u32[]{:S(2)}) collective-permute-start(f32[64,256]{1,0:T(8,128)S(1)} %slice.22), channel_id=1, source_target_pairs={{0,4},{4,8},{8,12},{1,5},{5,9},{9,13},{2,6},{6,10},{10,14},{3,7},{... | collective-permute-start | bytes 196616 | tf_op jit(solution)/shard_map/ppermute | solution.py:314
  66.1 3.3 %collective-permute-start.6 = (bf16[32,8192]{1,0:T(8,128)(2,1)S(1)}, bf16[32,8192]{1,0:T(8,128)(2,1)S(1)}, u32[]{:S(2)}, u32[]{:S(2)}) collective-permute-start(bf16[32,8192]{1,0:T(8,128)(2,1)S(1)} %get-tuple-element.38), channel_id=1, source_target_pairs={{0,4},{4,0},{8,12},{12,8},{1,5},{5,1},{9,13},{13,9},{2,6},{6,2},{1... | collective-permute-start | bytes 1572872 | tf_op jit(solution)/shard_map/ppermute | solution.py:214
  72.5 2.8 %collective-permute-start.8 = (bf16[32,8192]{1,0:T(8,128)(2,1)S(1)}, bf16[32,8192]{1,0:T(8,128)(2,1)S(1)}, u32[]{:S(2)}, u32[]{:S(2)}) collective-permute-start(bf16[32,8192]{1,0:T(8,128)(2,1)S(1)} %get-tuple-element.43), channel_id=1, source_target_pairs={{0,4},{4,0},{8,12},{12,8},{1,5},{5,1},{9,13},{13,9},{2,6},{6,2},{1... | collective-permute-start | bytes 1572872 | tf_op jit(solution)/shard_map/ppermute | solution.py:214
  73.0 9.5 %collective-permute-start.7 = (bf16[16,8192]{1,0:T(8,128)(2,1)S(1)}, bf16[16,8192]{1,0:T(8,128)(2,1)S(1)}, u32[]{:S(2)}, u32[]{:S(2)}) collective-permute-start(bf16[16,8192]{1,0:T(8,128)(2,1)S(1)} %slice.32), channel_id=1, source_target_pairs={{0,8},{4,12},{8,0},{12,4},{1,9},{5,13},{9,1},{13,5},{2,10},{6,14},... | collective-permute-start | bytes 786440 | tf_op jit(solution)/shard_map/ppermute | solution.py:214
  75.5 12.3 %collective-permute-start.9 = (bf16[16,8192]{1,0:T(8,128)(2,1)S(1)}, bf16[16,8192]{1,0:T(8,128)(2,1)S(1)}, u32[]{:S(2)}, u32[]{:S(2)}) collective-permute-start(bf16[16,8192]{1,0:T(8,128)(2,1)S(1)} %slice.31), channel_id=1, source_target_pairs={{0,8},{4,12},{8,0},{12,4},{1,9},{5,13},{9,1},{13,5},{2,10},{6,14},... | collective-permute-start | bytes 786440 | tf_op jit(solution)/shard_map/ppermute | solution.py:214

commit v5 on v4

--- a/solution.py
+++ b/solution.py
@@ -14,7 +14,7 @@
 COLS = 1024
 LANES = 128
 TILE = 256
-FIRST_COMPUTED, SECOND_COMPUTED = (1,), (1, 3)
+FIRST_COMPUTED, SECOND_COMPUTED = (2,), (1, 3)
 KERNEL_VMEM = 10 << 20
 SMALL_VMEM = 6 << 20
 INV_TWO_PI = 0.15915494309189535
@@ -340,7 +340,9 @@
         filtered, sent = lax.optimization_barrier((filtered, sent))
         received = swapped(sent, "epoch", epoch_bits[-1])
         pieces.append(kept + received.astype(F32))
-    return jnp.concatenate(pieces, axis=1)
+    first, second = pieces
+    result = lax.pad(first, jnp.zeros((), F32), ((0, 0, 0), (0, coeffs - half, 0)))
+    return lax.dynamic_update_slice(result, second, (0, half))
 
 
 def solution(mesh):

time: 89.2 us -> 88.5 us (level)
    concatenate x1 -> x0, other arithmetic: 1.04 us -> none  [local(): return jnp.concatenate(pieces, axis=1)]
    dynamic_update_slice x0 -> x1, other arithmetic: none -> 1.04 us  [local(): return lax.dynamic_update_slice(result, second, (0, half))]
  transfers between devices with their start and end apart: 10 -> 10, of which waited for: 7 -> 7; matrix products, arithmetic and copies ran while one was open for 0% -> 0% of each run, Pallas kernels for 18% -> 17%
where the time goes in v5:
time: 88.5 us; the launch traced here: 88.3 us
  Pallas kernels  47 us (53%)
  waiting for transfers between devices  23.9 us (27%)
  starting transfers between devices  15.6 us (18%)
  other arithmetic  1.4 us (2%)
    ppermute x9, waiting for transfers between devices, swapped(): return lax.ppermute(array, axis, [(i, i ^ bit) for i in range(size)])  23.9 us
    pallas_call x1, Pallas kernels, local(): pl.pallas_call(functools.partial(second_kernel, len(blocks)), grid=(steps...  23.5 us
    ppermute x9, starting transfers between devices, swapped(): return lax.ppermute(array, axis, [(i, i ^ bit) for i in range(size)])  14.4 us
    pallas_call x1, Pallas kernels, local(): pl.pallas_call(first_kernel, grid=(steps,), in_specs=[vmem] * 3 + [across...  14.2 us
    pallas_call x2, Pallas kernels, local(): pl.pallas_call(residual_kernel, in_specs=[vmem] * 2, out_specs=[vmem] * 2...  6.04 us
  transfers between devices with their start and end apart: 10, of which 7 were waited for; matrix products, arithmetic and copies ran while one was open for 0% of the time, Pallas kernels for 17%

profile of v5, /device:TPU:0, one launch (start us, length us, event | category | flops | bytes accessed | tf_op | source)
XLA Modules:
  0.0 88.3 jit_solution(12693998746110298062)
XLA Ops:
  0.0 1.7 %trig.1 = (bf16[1024,256]{1,0:T(8,128)(2,1)S(1)}, bf16[1024,512]{1,0:T(8,128)(2,1)S(1)}, f32[1024,128]{1,0:T(8,128)S(1)}) custom-call(s32[1,1024]{1,0:T(1,128)} %bitcast.6, f32[1,1024]{1,0:T(1,128)} %bitcast.7, f32[1,1024]{1,0:T(1,128)} %bitcast.8), custom_call_target="tpu_custom_call" | custom-call | flops 10485760 | bytes 12288 | tf_op jit(solution)/shard_map/trig/pallas_call | solution.py:245
  1.7 3.1 %collective-permute-start = (bf16[16,16384]{1,0:T(8,128)(2,1)}, bf16[16,16384]{1,0:T(8,128)(2,1)S(1)}, u32[]{:S(2)}, u32[]{:S(2)}) collective-permute-start(bf16[16,16384]{1,0:T(8,128)(2,1)} %refs_4_), channel_id=1, source_target_pairs={{0,8},{4,12},{8,0},{12,4},{1,9},{5,13},{9,1},{13,5},{2,10},{6,14},... | collective-permute-start | bytes 1572872 | tf_op jit(solution)/shard_map/ppermute | solution.py:214
  4.8 0.0 copy-start
  4.8 14.2 %design_first.1.old_ref.design_ref = bf16[8,1024,1024]{2,1,0:T(8,128)(2,1)S(1)} custom-call(bf16[1024,256]{1,0:T(8,128)(2,1)S(1)} %get-tuple-element.26.weights_ref, bf16[1024,512]{1,0:T(8,128)(2,1)S(1)} %get-tuple-element.27.trig_ref, f32[1024,128]{1,0:T(8,128)S(1)} %get-tuple-element.28.turns_ref, s32[1,16384]{1,0:T(1,128)} %bitcast.4, ...), custom_call_target="tpu_custom_call" | custom-call | flops 12884901888 | bytes 4194304 | tf_op jit(solution)/shard_map/design_first/pallas_call | solution.py:266
  19.0 0.0 copy-start.2
  19.0 0.0 copy-start.1
  19.0 0.0 collective-permute-done.refs_1_.refs_5_
  19.0 0.0 copy-done
  19.0 0.1 collective-permute-start.1
  19.1 0.5 collective-permute-start.2
  19.6 1.4 %collective-permute-done.1.refs_2_.refs_6_ = bf16[16,16384]{1,0:T(8,128)(2,1)S(1)} collective-permute-done((bf16[16,16384]{1,0:T(8,128)(2,1)S(1)}, bf16[16,16384]{1,0:T(8,128)(2,1)S(1)}, u32[]{:S(2)}, u32[]{:S(2)}) %collective-permute-start.1) | collective-permute-done | bytes 524320 | tf_op jit(solution)/shard_map/ppermute | solution.py:214
  21.0 0.7 collective-permute-done.2.refs_3_.refs_7_
  21.7 23.5 %design_second.1 = (bf16[8,1024,1024]{2,1,0:T(8,128)(2,1)S(1)}, f32[64,1024]{1,0:T(8,128)S(1)}, bf16[64,1024]{1,0:T(8,128)(2,1)S(1)}) custom-call(bf16[1024,256]{1,0:T(8,128)(2,1)S(1)} %get-tuple-element.26.weights_ref, bf16[1024,512]{1,0:T(8,128)(2,1)S(1)} %get-tuple-element.27.trig_ref, f32[1024,128]{1,0:T(8,128)S(1)} %get-tuple-element.28.turns_ref, ...), custom_call_target="tpu_custom_call" | custom-call | flops 15032385536 | bytes 37748736 | tf_op jit(solution)/shard_map/design_second/pallas_call | solution.py:284
  45.3 1.6 %collective-permute-start.3 = (bf16[64,1024]{1,0:T(8,128)(2,1)S(1)}, bf16[64,1024]{1,0:T(8,128)(2,1)S(1)}, u32[]{:S(2)}, u32[]{:S(2)}) collective-permute-start(bf16[64,1024]{1,0:T(8,128)(2,1)S(1)} %get-tuple-element.34), channel_id=1, source_target_pairs={{0,1},{1,0},{2,3},{3,2},{4,5},{5,4},{6,7},{7,6},{8,9},{9,8},{10,11... | collective-permute-start | bytes 393224 | tf_op jit(solution)/shard_map/ppermute | solution.py:214
  46.9 4.0 %collective-permute-done.3 = bf16[64,1024]{1,0:T(8,128)(2,1)S(1)} collective-permute-done((bf16[64,1024]{1,0:T(8,128)(2,1)S(1)}, bf16[64,1024]{1,0:T(8,128)(2,1)S(1)}, u32[]{:S(2)}, u32[]{:S(2)}) %collective-permute-start.3) | collective-permute-done | bytes 131104 | tf_op jit(solution)/shard_map/ppermute | solution.py:214
  50.9 2.7 %collective-permute-start.4 = (bf16[64,1024]{1,0:T(8,128)(2,1)S(1)}, bf16[64,1024]{1,0:T(8,128)(2,1)S(1)}, u32[]{:S(2)}, u32[]{:S(2)}) collective-permute-start(bf16[64,1024]{1,0:T(8,128)(2,1)S(1)} %fusion), channel_id=1, source_target_pairs={{0,2},{1,3},{2,0},{3,1},{4,6},{5,7},{6,4},{7,5},{8,10},{9,11},{10,... | collective-permute-start | bytes 393224 | tf_op jit(solution)/shard_map/ppermute | solution.py:214
  53.6 5.8 %collective-permute-done.4 = bf16[64,1024]{1,0:T(8,128)(2,1)S(1)} collective-permute-done((bf16[64,1024]{1,0:T(8,128)(2,1)S(1)}, bf16[64,1024]{1,0:T(8,128)(2,1)S(1)}, u32[]{:S(2)}, u32[]{:S(2)}) %collective-permute-start.4) | collective-permute-done | bytes 131104 | tf_op jit(solution)/shard_map/ppermute | solution.py:214
  59.4 1.3 %collective-permute-start.5 = (f32[64,256]{1,0:T(8,128)S(1)}, f32[64,256]{1,0:T(8,128)S(1)}, u32[]{:S(2)}, u32[]{:S(2)}) collective-permute-start(f32[64,256]{1,0:T(8,128)S(1)} %slice.22), channel_id=1, source_target_pairs={{0,4},{4,8},{8,12},{1,5},{5,9},{9,13},{2,6},{6,10},{10,14},{3,7},{... | collective-permute-start | bytes 196616 | tf_op jit(solution)/shard_map/ppermute | solution.py:314
  60.7 0.0 copy-done.2
  60.8 0.0 copy-done.1
  60.8 0.9 %tables.1 = (bf16[4,512,256]{2,1,0:T(8,128)(2,1)S(1)}, bf16[4,512,256]{2,1,0:T(8,128)(2,1)S(1)}) custom-call(s32[4]{0:T(128)S(1)} %copy-done.1, f32[8,512]{1,0:T(8,128)S(1)} %pad.5.bank_ref), custom_call_target="tpu_custom_call" | custom-call | flops 10485760 | bytes 2097152 | tf_op jit(solution)/shard_map/tables/pallas_call | solution.py:235
  61.7 0.0 collective-permute-done.5.before_ref
  61.7 0.7 filter.1.filtered_ref
  62.4 3.0 %residual.2 = (f32[32,8192]{1,0:T(8,128)S(1)}, bf16[32,8192]{1,0:T(8,128)(2,1)S(1)}) custom-call(bf16[64,1024]{1,0:T(8,128)(2,1)S(1)} %filter.1.filtered_ref, bf16[8,1024,1024]{2,1,0:T(8,128)(2,1)S(1)} %design_first.1.old_ref.design_ref), custom_call_target="tpu_custom_call" | custom-call | flops 1073741824 | bytes 3145728 | tf_op jit(solution)/shard_map/residual/pallas_call | solution.py:327
  65.4 1.8 %collective-permute-start.6 = (bf16[32,8192]{1,0:T(8,128)(2,1)S(1)}, bf16[32,8192]{1,0:T(8,128)(2,1)S(1)}, u32[]{:S(2)}, u32[]{:S(2)}) collective-permute-start(bf16[32,8192]{1,0:T(8,128)(2,1)S(1)} %get-tuple-element.38), channel_id=1, source_target_pairs={{0,4},{4,0},{8,12},{12,8},{1,5},{5,1},{9,13},{13,9},{2,6},{6,2},{1... | collective-permute-start | bytes 1572872 | tf_op jit(solution)/shard_map/ppermute | solution.py:214
  67.2 1.5 %collective-permute-done.6 = bf16[32,8192]{1,0:T(8,128)(2,1)S(1)} collective-permute-done((bf16[32,8192]{1,0:T(8,128)(2,1)S(1)}, bf16[32,8192]{1,0:T(8,128)(2,1)S(1)}, u32[]{:S(2)}, u32[]{:S(2)}) %collective-permute-start.6) | collective-permute-done | bytes 524320 | tf_op jit(solution)/shard_map/ppermute | solution.py:214
  68.7 0.1 convert_add_fusion.1
  68.8 3.0 %residual.3 = (f32[32,8192]{1,0:T(8,128)S(1)}, bf16[32,8192]{1,0:T(8,128)(2,1)S(1)}) custom-call(bf16[64,1024]{1,0:T(8,128)(2,1)S(1)} %filter.1.filtered_ref, bf16[8,1024,1024]{2,1,0:T(8,128)(2,1)S(1)} %get-tuple-element.41.design_ref), custom_call_target="tpu_custom_call" | custom-call | flops 1073741824 | bytes 3145728 | tf_op jit(solution)/shard_map/residual/pallas_call | solution.py:327
  71.9 0.4 collective-permute-start.8
  72.3 2.4 %collective-permute-start.7 = (bf16[16,8192]{1,0:T(8,128)(2,1)S(1)}, bf16[16,8192]{1,0:T(8,128)(2,1)S(1)}, u32[]{:S(2)}, u32[]{:S(2)}) collective-permute-start(bf16[16,8192]{1,0:T(8,128)(2,1)S(1)} %slice.32), channel_id=1, source_target_pairs={{0,8},{4,12},{8,0},{12,4},{1,9},{5,13},{9,1},{13,5},{2,10},{6,14},... | collective-permute-start | bytes 786440 | tf_op jit(solution)/shard_map/ppermute | solution.py:214
  74.7 0.0 collective-permute-done.8
  74.7 0.1 convert_add_fusion
  74.8 1.8 %collective-permute-start.9 = (bf16[16,8192]{1,0:T(8,128)(2,1)S(1)}, bf16[16,8192]{1,0:T(8,128)(2,1)S(1)}, u32[]{:S(2)}, u32[]{:S(2)}) collective-permute-start(bf16[16,8192]{1,0:T(8,128)(2,1)S(1)} %slice.31), channel_id=1, source_target_pairs={{0,8},{4,12},{8,0},{12,4},{1,9},{5,13},{9,1},{13,5},{2,10},{6,14},... | collective-permute-start | bytes 786440 | tf_op jit(solution)/shard_map/ppermute | solution.py:214
  76.7 5.2 %collective-permute-done.7 = bf16[16,8192]{1,0:T(8,128)(2,1)S(1)} collective-permute-done((bf16[16,8192]{1,0:T(8,128)(2,1)S(1)}, bf16[16,8192]{1,0:T(8,128)(2,1)S(1)}, u32[]{:S(2)}, u32[]{:S(2)}) %collective-permute-start.7) | collective-permute-done | bytes 262176 | tf_op jit(solution)/shard_map/ppermute | solution.py:214
  81.9 5.3 %collective-permute-done.9 = bf16[16,8192]{1,0:T(8,128)(2,1)S(1)} collective-permute-done((bf16[16,8192]{1,0:T(8,128)(2,1)S(1)}, bf16[16,8192]{1,0:T(8,128)(2,1)S(1)}, u32[]{:S(2)}, u32[]{:S(2)}) %collective-permute-start.9) | collective-permute-done | bytes 262176 | tf_op jit(solution)/shard_map/ppermute | solution.py:214
  87.2 0.1 slice_add_fusion
  87.2 1.0 %pad_maximum_fusion = f32[16,16384]{1,0:T(8,128)} fusion(f32[16,8192]{1,0:T(8,128)S(1)} %slice_add_fusion, f32[16,8192]{1,0:T(8,128)S(1)} %slice_add_fusion.1), kind=kLoop, calls=%fused_computation | loop fusion | flops 262144 | bytes 2097152 | tf_op jit(solution)/shard_map/dynamic_update_slice | solution.py:345
  (7 shorter events, 0.2 us)
Async XLA Ops:
  1.7 17.3 %collective-permute-start = (bf16[16,16384]{1,0:T(8,128)(2,1)}, bf16[16,16384]{1,0:T(8,128)(2,1)S(1)}, u32[]{:S(2)}, u32[]{:S(2)}) collective-permute-start(bf16[16,16384]{1,0:T(8,128)(2,1)} %refs_4_), channel_id=1, source_target_pairs={{0,8},{4,12},{8,0},{12,4},{1,9},{5,13},{9,1},{13,5},{2,10},{6,14},... | collective-permute-start | bytes 1572872 | tf_op jit(solution)/shard_map/ppermute | solution.py:214
  4.8 14.2 %copy-start = (bf16[16,16384]{1,0:T(8,128)(2,1)S(1)}, bf16[16,16384]{1,0:T(8,128)(2,1)}, u32[]{:S(2)}) copy-start(bf16[16,16384]{1,0:T(8,128)(2,1)} %refs_4_) | copy-start | bytes 1572868
  19.0 41.8 %copy-start.2 = (f32[8,255]{1,0:T(8,128)S(1)}, f32[8,255]{1,0:T(8,128)}, u32[]{:S(2)}) copy-start(f32[8,255]{1,0:T(8,128)} %param.14) | copy-start | bytes 24484
  19.0 41.8 %copy-start.1 = (s32[4]{0:T(128)S(1)}, s32[4]{0:T(128)}, u32[]{:S(2)}) copy-start(s32[4]{0:T(128)} %seg_ref.1) | copy-start | bytes 52
  19.0 2.0 %collective-permute-start.1 = (bf16[16,16384]{1,0:T(8,128)(2,1)S(1)}, bf16[16,16384]{1,0:T(8,128)(2,1)S(1)}, u32[]{:S(2)}, u32[]{:S(2)}) collective-permute-start(bf16[16,16384]{1,0:T(8,128)(2,1)S(1)} %copy-done), channel_id=1, source_target_pairs={{0,4},{4,0},{8,12},{12,8},{1,5},{5,1},{9,13},{13,9},{2,6},{6,2},{1... | collective-permute-start | bytes 1572872 | tf_op jit(solution)/shard_map/ppermute | solution.py:214
  19.1 2.6 %collective-permute-start.2 = (bf16[16,16384]{1,0:T(8,128)(2,1)S(1)}, bf16[16,16384]{1,0:T(8,128)(2,1)S(1)}, u32[]{:S(2)}, u32[]{:S(2)}) collective-permute-start(bf16[16,16384]{1,0:T(8,128)(2,1)S(1)} %collective-permute-done.refs_1_.refs_5_), channel_id=1, source_target_pairs={{0,4},{4,0},{8,12},{12,8},{1,5},{5,1},{9,13},{13,9},{2,6},{6,2},{1... | collective-permute-start | bytes 1572872 | tf_op jit(solution)/shard_map/ppermute | solution.py:214
  45.3 5.6 %collective-permute-start.3 = (bf16[64,1024]{1,0:T(8,128)(2,1)S(1)}, bf16[64,1024]{1,0:T(8,128)(2,1)S(1)}, u32[]{:S(2)}, u32[]{:S(2)}) collective-permute-start(bf16[64,1024]{1,0:T(8,128)(2,1)S(1)} %get-tuple-element.34), channel_id=1, source_target_pairs={{0,1},{1,0},{2,3},{3,2},{4,5},{5,4},{6,7},{7,6},{8,9},{9,8},{10,11... | collective-permute-start | bytes 393224 | tf_op jit(solution)/shard_map/ppermute | solution.py:214
  50.9 8.5 %collective-permute-start.4 = (bf16[64,1024]{1,0:T(8,128)(2,1)S(1)}, bf16[64,1024]{1,0:T(8,128)(2,1)S(1)}, u32[]{:S(2)}, u32[]{:S(2)}) collective-permute-start(bf16[64,1024]{1,0:T(8,128)(2,1)S(1)} %fusion), channel_id=1, source_target_pairs={{0,2},{1,3},{2,0},{3,1},{4,6},{5,7},{6,4},{7,5},{8,10},{9,11},{10,... | collective-permute-start | bytes 393224 | tf_op jit(solution)/shard_map/ppermute | solution.py:214
  59.4 2.2 %collective-permute-start.5 = (f32[64,256]{1,0:T(8,128)S(1)}, f32[64,256]{1,0:T(8,128)S(1)}, u32[]{:S(2)}, u32[]{:S(2)}) collective-permute-start(f32[64,256]{1,0:T(8,128)S(1)} %slice.22), channel_id=1, source_target_pairs={{0,4},{4,8},{8,12},{1,5},{5,9},{9,13},{2,6},{6,10},{10,14},{3,7},{... | collective-permute-start | bytes 196616 | tf_op jit(solution)/shard_map/ppermute | solution.py:314
  65.4 3.3 %collective-permute-start.6 = (bf16[32,8192]{1,0:T(8,128)(2,1)S(1)}, bf16[32,8192]{1,0:T(8,128)(2,1)S(1)}, u32[]{:S(2)}, u32[]{:S(2)}) collective-permute-start(bf16[32,8192]{1,0:T(8,128)(2,1)S(1)} %get-tuple-element.38), channel_id=1, source_target_pairs={{0,4},{4,0},{8,12},{12,8},{1,5},{5,1},{9,13},{13,9},{2,6},{6,2},{1... | collective-permute-start | bytes 1572872 | tf_op jit(solution)/shard_map/ppermute | solution.py:214
  71.9 2.8 %collective-permute-start.8 = (bf16[32,8192]{1,0:T(8,128)(2,1)S(1)}, bf16[32,8192]{1,0:T(8,128)(2,1)S(1)}, u32[]{:S(2)}, u32[]{:S(2)}) collective-permute-start(bf16[32,8192]{1,0:T(8,128)(2,1)S(1)} %get-tuple-element.43), channel_id=1, source_target_pairs={{0,4},{4,0},{8,12},{12,8},{1,5},{5,1},{9,13},{13,9},{2,6},{6,2},{1... | collective-permute-start | bytes 1572872 | tf_op jit(solution)/shard_map/ppermute | solution.py:214
  72.3 9.5 %collective-permute-start.7 = (bf16[16,8192]{1,0:T(8,128)(2,1)S(1)}, bf16[16,8192]{1,0:T(8,128)(2,1)S(1)}, u32[]{:S(2)}, u32[]{:S(2)}) collective-permute-start(bf16[16,8192]{1,0:T(8,128)(2,1)S(1)} %slice.32), channel_id=1, source_target_pairs={{0,8},{4,12},{8,0},{12,4},{1,9},{5,13},{9,1},{13,5},{2,10},{6,14},... | collective-permute-start | bytes 786440 | tf_op jit(solution)/shard_map/ppermute | solution.py:214
  74.8 12.3 %collective-permute-start.9 = (bf16[16,8192]{1,0:T(8,128)(2,1)S(1)}, bf16[16,8192]{1,0:T(8,128)(2,1)S(1)}, u32[]{:S(2)}, u32[]{:S(2)}) collective-permute-start(bf16[16,8192]{1,0:T(8,128)(2,1)S(1)} %slice.31), channel_id=1, source_target_pairs={{0,8},{4,12},{8,0},{12,4},{1,9},{5,13},{9,1},{13,5},{2,10},{6,14},... | collective-permute-start | bytes 786440 | tf_op jit(solution)/shard_map/ppermute | solution.py:214

commit v6 on v5

--- a/solution.py
+++ b/solution.py
@@ -14,7 +14,7 @@
 COLS = 1024
 LANES = 128
 TILE = 256
-FIRST_COMPUTED, SECOND_COMPUTED = (2,), (1, 3)
+FIRST_COMPUTED, SECOND_COMPUTED = (2,), (0, 3)
 KERNEL_VMEM = 10 << 20
 SMALL_VMEM = 6 << 20
 INV_TWO_PI = 0.15915494309189535
@@ -263,6 +263,7 @@
     for bit in reversed(epoch_bits[1:]):
         blocks += [swapped(block, "epoch", bit) for block in blocks]
 
+    near = swapped(probes, "epoch", epoch_bits[0])
     design_1 = pl.pallas_call(
         first_kernel,
         grid=(steps,),
@@ -274,8 +275,8 @@
         compiler_params=pltpu.CompilerParams(vmem_limit_bytes=KERNEL_VMEM),
         name="design_first",
     )(*angular, codes, legendre)
-    blocks, design_1 = lax.optimization_barrier((blocks, design_1))
-    blocks = blocks + [swapped(block, "epoch", epoch_bits[0]) for block in blocks]
+    far, design_1 = lax.optimization_barrier((blocks[1:], design_1))
+    blocks = [probes, *far, near] + [swapped(block, "epoch", epoch_bits[0]) for block in far]
     count = own * len(blocks)
     if own % 16:
         blocks = [jnp.concatenate(blocks, axis=0)]

time: 88.5 us -> 88.7 us (level)
  transfers between devices with their start and end apart: 10 -> 10, of which waited for: 7 -> 6; matrix products, arithmetic and copies ran while one was open for 0% -> 0% of each run, Pallas kernels for 17% -> 17%
where the time goes in v6:
time: 88.7 us; the launch traced here: 88.5 us
  Pallas kernels  47.4 us (53%)
  waiting for transfers between devices  23.8 us (27%)
  starting transfers between devices  15.6 us (18%)
  other arithmetic  1.4 us (2%)
    pallas_call x1, Pallas kernels, local(): pl.pallas_call(functools.partial(second_kernel, len(blocks)), grid=(steps...  23.9 us
    ppermute x9, waiting for transfers between devices, swapped(): return lax.ppermute(array, axis, [(i, i ^ bit) for i in range(size)])  23.8 us
    ppermute x9, starting transfers between devices, swapped(): return lax.ppermute(array, axis, [(i, i ^ bit) for i in range(size)])  14.4 us
    pallas_call x1, Pallas kernels, local(): pl.pallas_call(first_kernel, grid=(steps,), in_specs=[vmem] * 3 + [across...  14.2 us
    pallas_call x2, Pallas kernels, local(): pl.pallas_call(residual_kernel, in_specs=[vmem] * 2, out_specs=[vmem] * 2...  6.04 us
  transfers between devices with their start and end apart: 10, of which 6 were waited for; matrix products, arithmetic and copies ran while one was open for 0% of the time, Pallas kernels for 17%

profile of v6, /device:TPU:0, one launch (start us, length us, event | category | flops | bytes accessed | tf_op | source)
XLA Modules:
  0.0 88.5 jit_solution(16076328225471115693)
XLA Ops:
  0.0 1.7 %trig.1 = (bf16[1024,256]{1,0:T(8,128)(2,1)S(1)}, bf16[1024,512]{1,0:T(8,128)(2,1)S(1)}, f32[1024,128]{1,0:T(8,128)S(1)}) custom-call(s32[1,1024]{1,0:T(1,128)} %bitcast.6, f32[1,1024]{1,0:T(1,128)} %bitcast.7, f32[1,1024]{1,0:T(1,128)} %bitcast.8), custom_call_target="tpu_custom_call" | custom-call | flops 10485760 | bytes 12288 | tf_op jit(solution)/shard_map/trig/pallas_call | solution.py:245
  1.7 3.1 %collective-permute-start = (bf16[16,16384]{1,0:T(8,128)(2,1)}, bf16[16,16384]{1,0:T(8,128)(2,1)S(1)}, u32[]{:S(2)}, u32[]{:S(2)}) collective-permute-start(bf16[16,16384]{1,0:T(8,128)(2,1)} %refs_4_), channel_id=1, source_target_pairs={{0,8},{4,12},{8,0},{12,4},{1,9},{5,13},{9,1},{13,5},{2,10},{6,14},... | collective-permute-start | bytes 1572872 | tf_op jit(solution)/shard_map/ppermute | solution.py:214
  4.8 0.0 collective-permute-start.1
  4.8 0.0 copy-start
  4.8 14.2 %design_first.1.old_ref.design_ref = bf16[8,1024,1024]{2,1,0:T(8,128)(2,1)S(1)} custom-call(bf16[1024,256]{1,0:T(8,128)(2,1)S(1)} %get-tuple-element.25.weights_ref, bf16[1024,512]{1,0:T(8,128)(2,1)S(1)} %get-tuple-element.26.trig_ref, f32[1024,128]{1,0:T(8,128)S(1)} %get-tuple-element.27.turns_ref, s32[1,16384]{1,0:T(1,128)} %bitcast.4, ...), custom_call_target="tpu_custom_call" | custom-call | flops 12884901888 | bytes 4194304 | tf_op jit(solution)/shard_map/design_first/pallas_call | solution.py:267
  19.0 0.0 copy-start.2
  19.0 0.0 copy-start.1
  19.0 0.0 collective-permute-done.refs_1_.refs_5_
  19.0 0.6 collective-permute-start.2
  19.6 0.0 collective-permute-done.1.refs_2_.refs_6_
  19.6 1.5 %collective-permute-done.2.refs_3_.refs_7_ = bf16[16,16384]{1,0:T(8,128)(2,1)S(1)} collective-permute-done((bf16[16,16384]{1,0:T(8,128)(2,1)S(1)}, bf16[16,16384]{1,0:T(8,128)(2,1)S(1)}, u32[]{:S(2)}, u32[]{:S(2)}) %collective-permute-start.2) | collective-permute-done | bytes 524320 | tf_op jit(solution)/shard_map/ppermute | solution.py:214
  21.1 0.0 copy-done
  21.1 23.9 %design_second.1 = (bf16[8,1024,1024]{2,1,0:T(8,128)(2,1)S(1)}, f32[64,1024]{1,0:T(8,128)S(1)}, bf16[64,1024]{1,0:T(8,128)(2,1)S(1)}) custom-call(bf16[1024,256]{1,0:T(8,128)(2,1)S(1)} %get-tuple-element.25.weights_ref, bf16[1024,512]{1,0:T(8,128)(2,1)S(1)} %get-tuple-element.26.trig_ref, f32[1024,128]{1,0:T(8,128)S(1)} %get-tuple-element.27.turns_ref, ...), custom_call_target="tpu_custom_call" | custom-call | flops 15032385536 | bytes 37748736 | tf_op jit(solution)/shard_map/design_second/pallas_call | solution.py:285
  45.0 1.6 %collective-permute-start.3 = (bf16[64,1024]{1,0:T(8,128)(2,1)S(1)}, bf16[64,1024]{1,0:T(8,128)(2,1)S(1)}, u32[]{:S(2)}, u32[]{:S(2)}) collective-permute-start(bf16[64,1024]{1,0:T(8,128)(2,1)S(1)} %get-tuple-element.32), channel_id=1, source_target_pairs={{0,1},{1,0},{2,3},{3,2},{4,5},{5,4},{6,7},{7,6},{8,9},{9,8},{10,11... | collective-permute-start | bytes 393224 | tf_op jit(solution)/shard_map/ppermute | solution.py:214
  46.7 4.2 %collective-permute-done.3 = bf16[64,1024]{1,0:T(8,128)(2,1)S(1)} collective-permute-done((bf16[64,1024]{1,0:T(8,128)(2,1)S(1)}, bf16[64,1024]{1,0:T(8,128)(2,1)S(1)}, u32[]{:S(2)}, u32[]{:S(2)}) %collective-permute-start.3) | collective-permute-done | bytes 131104 | tf_op jit(solution)/shard_map/ppermute | solution.py:214
  50.9 2.7 %collective-permute-start.4 = (bf16[64,1024]{1,0:T(8,128)(2,1)S(1)}, bf16[64,1024]{1,0:T(8,128)(2,1)S(1)}, u32[]{:S(2)}, u32[]{:S(2)}) collective-permute-start(bf16[64,1024]{1,0:T(8,128)(2,1)S(1)} %fusion), channel_id=1, source_target_pairs={{0,2},{1,3},{2,0},{3,1},{4,6},{5,7},{6,4},{7,5},{8,10},{9,11},{10,... | collective-permute-start | bytes 393224 | tf_op jit(solution)/shard_map/ppermute | solution.py:214
  53.6 6.0 %collective-permute-done.4 = bf16[64,1024]{1,0:T(8,128)(2,1)S(1)} collective-permute-done((bf16[64,1024]{1,0:T(8,128)(2,1)S(1)}, bf16[64,1024]{1,0:T(8,128)(2,1)S(1)}, u32[]{:S(2)}, u32[]{:S(2)}) %collective-permute-start.4) | collective-permute-done | bytes 131104 | tf_op jit(solution)/shard_map/ppermute | solution.py:214
  59.7 1.3 %collective-permute-start.5 = (f32[64,256]{1,0:T(8,128)S(1)}, f32[64,256]{1,0:T(8,128)S(1)}, u32[]{:S(2)}, u32[]{:S(2)}) collective-permute-start(f32[64,256]{1,0:T(8,128)S(1)} %slice.22), channel_id=1, source_target_pairs={{0,4},{4,8},{8,12},{1,5},{5,9},{9,13},{2,6},{6,10},{10,14},{3,7},{... | collective-permute-start | bytes 196616 | tf_op jit(solution)/shard_map/ppermute | solution.py:315
  61.0 0.0 copy-done.2
  61.0 0.0 copy-done.1
  61.0 0.9 %tables.1 = (bf16[4,512,256]{2,1,0:T(8,128)(2,1)S(1)}, bf16[4,512,256]{2,1,0:T(8,128)(2,1)S(1)}) custom-call(s32[4]{0:T(128)S(1)} %copy-done.1, f32[8,512]{1,0:T(8,128)S(1)} %pad.5.bank_ref), custom_call_target="tpu_custom_call" | custom-call | flops 10485760 | bytes 2097152 | tf_op jit(solution)/shard_map/tables/pallas_call | solution.py:235
  61.9 0.0 collective-permute-done.5.before_ref
  61.9 0.7 filter.1.filtered_ref
  62.6 3.0 %residual.2 = (f32[32,8192]{1,0:T(8,128)S(1)}, bf16[32,8192]{1,0:T(8,128)(2,1)S(1)}) custom-call(bf16[64,1024]{1,0:T(8,128)(2,1)S(1)} %filter.1.filtered_ref, bf16[8,1024,1024]{2,1,0:T(8,128)(2,1)S(1)} %design_first.1.old_ref.design_ref), custom_call_target="tpu_custom_call" | custom-call | flops 1073741824 | bytes 3145728 | tf_op jit(solution)/shard_map/residual/pallas_call | solution.py:328
  65.6 1.8 %collective-permute-start.6 = (bf16[32,8192]{1,0:T(8,128)(2,1)S(1)}, bf16[32,8192]{1,0:T(8,128)(2,1)S(1)}, u32[]{:S(2)}, u32[]{:S(2)}) collective-permute-start(bf16[32,8192]{1,0:T(8,128)(2,1)S(1)} %get-tuple-element.36), channel_id=1, source_target_pairs={{0,4},{4,0},{8,12},{12,8},{1,5},{5,1},{9,13},{13,9},{2,6},{6,2},{1... | collective-permute-start | bytes 1572872 | tf_op jit(solution)/shard_map/ppermute | solution.py:214
  67.4 1.5 %collective-permute-done.6 = bf16[32,8192]{1,0:T(8,128)(2,1)S(1)} collective-permute-done((bf16[32,8192]{1,0:T(8,128)(2,1)S(1)}, bf16[32,8192]{1,0:T(8,128)(2,1)S(1)}, u32[]{:S(2)}, u32[]{:S(2)}) %collective-permute-start.6) | collective-permute-done | bytes 524320 | tf_op jit(solution)/shard_map/ppermute | solution.py:214
  68.9 0.1 convert_add_fusion.1
  69.1 3.0 %residual.3 = (f32[32,8192]{1,0:T(8,128)S(1)}, bf16[32,8192]{1,0:T(8,128)(2,1)S(1)}) custom-call(bf16[64,1024]{1,0:T(8,128)(2,1)S(1)} %filter.1.filtered_ref, bf16[8,1024,1024]{2,1,0:T(8,128)(2,1)S(1)} %get-tuple-element.39.design_ref), custom_call_target="tpu_custom_call" | custom-call | flops 1073741824 | bytes 3145728 | tf_op jit(solution)/shard_map/residual/pallas_call | solution.py:328
  72.1 0.4 collective-permute-start.8
  72.5 2.4 %collective-permute-start.7 = (bf16[16,8192]{1,0:T(8,128)(2,1)S(1)}, bf16[16,8192]{1,0:T(8,128)(2,1)S(1)}, u32[]{:S(2)}, u32[]{:S(2)}) collective-permute-start(bf16[16,8192]{1,0:T(8,128)(2,1)S(1)} %slice.32), channel_id=1, source_target_pairs={{0,8},{4,12},{8,0},{12,4},{1,9},{5,13},{9,1},{13,5},{2,10},{6,14},... | collective-permute-start | bytes 786440 | tf_op jit(solution)/shard_map/ppermute | solution.py:214
  74.9 0.0 collective-permute-done.8
  74.9 0.1 convert_add_fusion
  75.0 1.8 %collective-permute-start.9 = (bf16[16,8192]{1,0:T(8,128)(2,1)S(1)}, bf16[16,8192]{1,0:T(8,128)(2,1)S(1)}, u32[]{:S(2)}, u32[]{:S(2)}) collective-permute-start(bf16[16,8192]{1,0:T(8,128)(2,1)S(1)} %slice.31), channel_id=1, source_target_pairs={{0,8},{4,12},{8,0},{12,4},{1,9},{5,13},{9,1},{13,5},{2,10},{6,14},... | collective-permute-start | bytes 786440 | tf_op jit(solution)/shard_map/ppermute | solution.py:214
  76.9 5.2 %collective-permute-done.7 = bf16[16,8192]{1,0:T(8,128)(2,1)S(1)} collective-permute-done((bf16[16,8192]{1,0:T(8,128)(2,1)S(1)}, bf16[16,8192]{1,0:T(8,128)(2,1)S(1)}, u32[]{:S(2)}, u32[]{:S(2)}) %collective-permute-start.7) | collective-permute-done | bytes 262176 | tf_op jit(solution)/shard_map/ppermute | solution.py:214
  82.1 5.3 %collective-permute-done.9 = bf16[16,8192]{1,0:T(8,128)(2,1)S(1)} collective-permute-done((bf16[16,8192]{1,0:T(8,128)(2,1)S(1)}, bf16[16,8192]{1,0:T(8,128)(2,1)S(1)}, u32[]{:S(2)}, u32[]{:S(2)}) %collective-permute-start.9) | collective-permute-done | bytes 262176 | tf_op jit(solution)/shard_map/ppermute | solution.py:214
  87.4 0.1 slice_add_fusion
  87.4 1.0 %pad_maximum_fusion = f32[16,16384]{1,0:T(8,128)} fusion(f32[16,8192]{1,0:T(8,128)S(1)} %slice_add_fusion, f32[16,8192]{1,0:T(8,128)S(1)} %slice_add_fusion.1), kind=kLoop, calls=%fused_computation | loop fusion | flops 262144 | bytes 2097152 | tf_op jit(solution)/shard_map/dynamic_update_slice | solution.py:346
  (7 shorter events, 0.2 us)
Async XLA Ops:
  1.7 17.3 %collective-permute-start = (bf16[16,16384]{1,0:T(8,128)(2,1)}, bf16[16,16384]{1,0:T(8,128)(2,1)S(1)}, u32[]{:S(2)}, u32[]{:S(2)}) collective-permute-start(bf16[16,16384]{1,0:T(8,128)(2,1)} %refs_4_), channel_id=1, source_target_pairs={{0,8},{4,12},{8,0},{12,4},{1,9},{5,13},{9,1},{13,5},{2,10},{6,14},... | collective-permute-start | bytes 1572872 | tf_op jit(solution)/shard_map/ppermute | solution.py:214
  4.8 14.8 %collective-permute-start.1 = (bf16[16,16384]{1,0:T(8,128)(2,1)}, bf16[16,16384]{1,0:T(8,128)(2,1)S(1)}, u32[]{:S(2)}, u32[]{:S(2)}) collective-permute-start(bf16[16,16384]{1,0:T(8,128)(2,1)} %refs_4_), channel_id=1, source_target_pairs={{0,4},{4,0},{8,12},{12,8},{1,5},{5,1},{9,13},{13,9},{2,6},{6,2},{1... | collective-permute-start | bytes 1572872 | tf_op jit(solution)/shard_map/ppermute | solution.py:214
  4.8 16.4 %copy-start = (bf16[16,16384]{1,0:T(8,128)(2,1)S(1)}, bf16[16,16384]{1,0:T(8,128)(2,1)}, u32[]{:S(2)}) copy-start(bf16[16,16384]{1,0:T(8,128)(2,1)} %refs_4_) | copy-start | bytes 1572868
  19.0 42.0 %copy-start.2 = (f32[8,255]{1,0:T(8,128)S(1)}, f32[8,255]{1,0:T(8,128)}, u32[]{:S(2)}) copy-start(f32[8,255]{1,0:T(8,128)} %param.14) | copy-start | bytes 24484
  19.0 42.0 %copy-start.1 = (s32[4]{0:T(128)S(1)}, s32[4]{0:T(128)}, u32[]{:S(2)}) copy-start(s32[4]{0:T(128)} %seg_ref.1) | copy-start | bytes 52
  19.0 2.1 %collective-permute-start.2 = (bf16[16,16384]{1,0:T(8,128)(2,1)S(1)}, bf16[16,16384]{1,0:T(8,128)(2,1)S(1)}, u32[]{:S(2)}, u32[]{:S(2)}) collective-permute-start(bf16[16,16384]{1,0:T(8,128)(2,1)S(1)} %collective-permute-done.refs_1_.refs_5_), channel_id=1, source_target_pairs={{0,4},{4,0},{8,12},{12,8},{1,5},{5,1},{9,13},{13,9},{2,6},{6,2},{1... | collective-permute-start | bytes 1572872 | tf_op jit(solution)/shard_map/ppermute | solution.py:214
  45.0 5.8 %collective-permute-start.3 = (bf16[64,1024]{1,0:T(8,128)(2,1)S(1)}, bf16[64,1024]{1,0:T(8,128)(2,1)S(1)}, u32[]{:S(2)}, u32[]{:S(2)}) collective-permute-start(bf16[64,1024]{1,0:T(8,128)(2,1)S(1)} %get-tuple-element.32), channel_id=1, source_target_pairs={{0,1},{1,0},{2,3},{3,2},{4,5},{5,4},{6,7},{7,6},{8,9},{9,8},{10,11... | collective-permute-start | bytes 393224 | tf_op jit(solution)/shard_map/ppermute | solution.py:214
  50.9 8.7 %collective-permute-start.4 = (bf16[64,1024]{1,0:T(8,128)(2,1)S(1)}, bf16[64,1024]{1,0:T(8,128)(2,1)S(1)}, u32[]{:S(2)}, u32[]{:S(2)}) collective-permute-start(bf16[64,1024]{1,0:T(8,128)(2,1)S(1)} %fusion), channel_id=1, source_target_pairs={{0,2},{1,3},{2,0},{3,1},{4,6},{5,7},{6,4},{7,5},{8,10},{9,11},{10,... | collective-permute-start | bytes 393224 | tf_op jit(solution)/shard_map/ppermute | solution.py:214
  59.7 2.2 %collective-permute-start.5 = (f32[64,256]{1,0:T(8,128)S(1)}, f32[64,256]{1,0:T(8,128)S(1)}, u32[]{:S(2)}, u32[]{:S(2)}) collective-permute-start(f32[64,256]{1,0:T(8,128)S(1)} %slice.22), channel_id=1, source_target_pairs={{0,4},{4,8},{8,12},{1,5},{5,9},{9,13},{2,6},{6,10},{10,14},{3,7},{... | collective-permute-start | bytes 196616 | tf_op jit(solution)/shard_map/ppermute | solution.py:315
  65.6 3.3 %collective-permute-start.6 = (bf16[32,8192]{1,0:T(8,128)(2,1)S(1)}, bf16[32,8192]{1,0:T(8,128)(2,1)S(1)}, u32[]{:S(2)}, u32[]{:S(2)}) collective-permute-start(bf16[32,8192]{1,0:T(8,128)(2,1)S(1)} %get-tuple-element.36), channel_id=1, source_target_pairs={{0,4},{4,0},{8,12},{12,8},{1,5},{5,1},{9,13},{13,9},{2,6},{6,2},{1... | collective-permute-start | bytes 1572872 | tf_op jit(solution)/shard_map/ppermute | solution.py:214
  72.1 2.8 %collective-permute-start.8 = (bf16[32,8192]{1,0:T(8,128)(2,1)S(1)}, bf16[32,8192]{1,0:T(8,128)(2,1)S(1)}, u32[]{:S(2)}, u32[]{:S(2)}) collective-permute-start(bf16[32,8192]{1,0:T(8,128)(2,1)S(1)} %get-tuple-element.41), channel_id=1, source_target_pairs={{0,4},{4,0},{8,12},{12,8},{1,5},{5,1},{9,13},{13,9},{2,6},{6,2},{1... | collective-permute-start | bytes 1572872 | tf_op jit(solution)/shard_map/ppermute | solution.py:214
  72.5 9.5 %collective-permute-start.7 = (bf16[16,8192]{1,0:T(8,128)(2,1)S(1)}, bf16[16,8192]{1,0:T(8,128)(2,1)S(1)}, u32[]{:S(2)}, u32[]{:S(2)}) collective-permute-start(bf16[16,8192]{1,0:T(8,128)(2,1)S(1)} %slice.32), channel_id=1, source_target_pairs={{0,8},{4,12},{8,0},{12,4},{1,9},{5,13},{9,1},{13,5},{2,10},{6,14},... | collective-permute-start | bytes 786440 | tf_op jit(solution)/shard_map/ppermute | solution.py:214
  75.0 12.3 %collective-permute-start.9 = (bf16[16,8192]{1,0:T(8,128)(2,1)S(1)}, bf16[16,8192]{1,0:T(8,128)(2,1)S(1)}, u32[]{:S(2)}, u32[]{:S(2)}) collective-permute-start(bf16[16,8192]{1,0:T(8,128)(2,1)S(1)} %slice.31), channel_id=1, source_target_pairs={{0,8},{4,12},{8,0},{12,4},{1,9},{5,13},{9,1},{13,5},{2,10},{6,14},... | collective-permute-start | bytes 786440 | tf_op jit(solution)/shard_map/ppermute | solution.py:214
